TPU v7x, 512 devices: a whole 4x8x8 slice. The times are simulated.
512 devices in a mesh: item: 16 (over y, core), user: 32 (over z, x).
Axes of the slice: x: 4, y: 8, z: 8, core: 2. Of those that a mesh axis runs over, the one named last changes fastest.
Arguments:
- item_factors: float32 [32768, 128], P('item')
- tile_lists: int32 [512, 16], P(('item', 'user')), may hold values from 0 to 255, as said below
- tile_weights: bfloat16 [512, 16, 128, 128], P(('item', 'user')), may hold values from 0 to 40
- user_factors: float32 [65536, 128], P(('item', 'user')), may hold values from -6 to 6
Outputs:
- new_factors: float32 [65536, 128], P(('item', 'user'))
Inputs may be any that keep to these rules, and one draw needn't show every extreme that they name: `tile_lists`: item shard s holds tiles s * 16 to (s + 1) * 16 - 1. Among the 16 slots of one device's blocks, at most 2 name tiles of one item shard, and for some shard exactly 2 do; a tile may be named more than once.
All inputs are finite; a program needn't handle non-finite values.
Results may differ from a plain program's by a relative error of at most 0.0024.
Values sent between devices are 32-bit elements; how exact they have to be, the bound alone decides.
No kernel may reach another device: no remote copies, remote signals or barrier semaphores. Data moves between devices by JAX's collectives and lax.ppermute only.
A program may use at most 64 MiB of HBM per device.

v0:
```python
import jax
import jax.numpy as jnp
from jax import lax
from jax.sharding import PartitionSpec as P

ITERS = 4


RIDGE_WEIGHT = 0.1
EPSILON = 1e-06
HIGHEST = lax.Precision.HIGHEST


def apply_system(vectors, tiles, weights, gram):
    scores = jnp.einsum("bur,bkir->bkui", vectors, tiles, precision=HIGHEST)
    spread = jnp.einsum("bkui,bkir->bur", scores * weights, tiles, precision=HIGHEST)
    return (
        spread
        + jnp.einsum("bur,rs->bus", vectors, gram, precision=HIGHEST)
        + RIDGE_WEIGHT * vectors
    )


def conjugate(start, tiles, weights, gram, steps):
    weights = weights.astype(jnp.float32)
    target = jnp.einsum("bkui,bkir->bur", 1.0 + weights, tiles, precision=HIGHEST)
    answer = start
    resid = target - apply_system(start, tiles, weights, gram)
    direction = resid
    norm_now = jnp.sum(resid * resid, axis=-1, keepdims=True)
    for step_index in range(steps):
        image = apply_system(direction, tiles, weights, gram)
        alpha = norm_now / (jnp.sum(direction * image, axis=-1, keepdims=True) + EPSILON)
        answer = answer + alpha * direction
        resid = resid - alpha * image
        norm_next = jnp.sum(resid * resid, axis=-1, keepdims=True)
        direction = resid + norm_next / (norm_now + EPSILON) * direction
        norm_now = norm_next
    return answer


def local(item_factors, tile_lists, tile_weights, user_factors):
    factor_rank = item_factors.shape[1]
    tile_side = tile_weights.shape[-1]
    blocks_here, slots_here = tile_lists.shape
    shard_rows = item_factors.shape[0]
    user_parts = lax.axis_size("user")
    share_rows = shard_rows // user_parts
    piece = lax.dynamic_slice_in_dim(
        item_factors, lax.axis_index("user") * share_rows, share_rows, 0
    )
    partial_gram = jnp.dot(piece.T, piece, precision=HIGHEST, preferred_element_type=jnp.float32)
    gram = lax.psum(partial_gram, ("item", "user"))
    tile_ids = tile_lists.reshape(-1)
    all_rows = lax.all_gather(item_factors, "item", axis=0, tiled=True)
    fetched = all_rows.reshape(-1, tile_side, factor_rank)[tile_ids]
    tiles = fetched.reshape(blocks_here, slots_here, tile_side, factor_rank)
    start = user_factors.reshape(blocks_here, tile_side, factor_rank)
    solved = conjugate(start, tiles, tile_weights, gram, ITERS)
    return solved.reshape(-1, factor_rank)


def solution(mesh):
    in_specs = (
        P("item", None),
        P(("item", "user"), None),
        P(("item", "user"), None, None, None),
        P(("item", "user"), None),
    )
    out_specs = P(("item", "user"), None)
    return jax.shard_map(local, mesh=mesh, in_specs=in_specs, out_specs=out_specs, check_vma=False)
```

profile of v0, /device:TPU:1, one launch (start us, length us, event | category | flops | bytes accessed | tf_op | source)
XLA Modules:
  0.0 362.3 jit_solution(888267724627594206)
XLA Ops:
  7.4 0.0 all-gather.2.cloned.1.call-start
  7.4 0.7 all-gather.2.cloned.1.call-update
  8.1 0.0 all-reduce.2.cloned.1.call-start
  8.1 1.8 fusion.22
  9.9 0.0 all-reduce.2.cloned.1.call-update
  9.9 0.7 fusion.24
  10.6 1.3 copy.24
  11.9 0.9 copy.33
  12.8 101.3 %all-gather.2.cloned.1.call-done = f32[32768,128]{1,0:T(8,128)} async-done(((f32[2048,128]{1,0:T(8,128)}), f32[32768,128]{1,0:T(8,128)}) %all-gather.2.cloned.1.call-update) | async-done | bytes 16777232 | tf_op jit(solution)/shard_map/all_gather | solution.py:55
  114.2 6.4 %gather_fusion = f32[16,128,128]{2,1,0:T(8,128)S(1)} fusion(f32[256,128,128]{2,1,0:T(8,128)} %bitcast.119, s32[1024]{0:T(1024)S(1)} %pad_clamp_fusion), kind=kCustom, calls=%fused_computation | custom fusion | bytes 2097216 | tf_op jit(solution)/shard_map/gather | solution.py:56
  120.6 1.8 fusion
  122.4 1.8 convolution_bitcast_fusion.10
  124.2 1.8 convolution_bitcast_fusion.11
  126.1 211.4 %all-reduce.2.cloned.1.call-done = f32[128,128]{1,0:T(8,128)} async-done(((f32[128,128]{1,0:T(8,128)}), f32[128,128]{1,0:T(8,128)}) %all-reduce.2.cloned.1.call-update) | async-done | bytes 65552 | tf_op jit(solution)/shard_map/psum | solution.py:53
  337.5 0.0 copy-start
  337.5 1.2 fusion.12
  338.7 1.0 fusion.1
  339.7 1.8 convolution_bitcast_fusion.8
  341.5 1.1 multiply_reduce_fusion.5
  342.7 1.0 fusion.2
  343.7 1.8 convolution_bitcast_fusion.7
  345.5 1.1 multiply_reduce_fusion.3
  346.8 1.2 fusion.3
  347.9 1.8 convolution_bitcast_fusion.6
  349.8 1.1 multiply_reduce_fusion.1
  351.0 1.0 fusion.4
  352.0 1.8 convolution_bitcast_fusion.5
  353.8 0.0 copy-done
  353.8 0.3 fusion.13
  354.2 0.7 copy.43
  (15 shorter events, 0.3 us)
Async XLA Ops:
  7.4 106.8 %all-gather.2.cloned.1.call-start = ((), (), s32[]{:S(2)}) async-start(), calls=%async_computation | async-start | bytes 17825792 | tf_op jit(solution)/shard_map/all_gather | solution.py:55
  8.1 329.4 %all-reduce.2.cloned.1.call-start = ((), (), s32[]{:S(2)}) async-start(), calls=%async_computation.1 | async-start | bytes 131072 | tf_op jit(solution)/shard_map/psum | solution.py:53
  337.5 16.3 %copy-start = (f32[128,128]{1,0:T(8,128)S(1)}, f32[128,128]{1,0:T(8,128)}, u32[]{:S(2)}) copy-start(f32[128,128]{1,0:T(8,128)} %all-reduce.2.cloned.1.call-done) | copy-start | bytes 196612
Sparse Core Ops, SparseCore 0:
  10.3 103.8 all-gather.1
Sparse Core Ops, SparseCore 1:
  13.6 323.9 all-reduce.1
where the time goes:
time: 363 us; the launch traced here: 362 us
  waiting for transfers between devices  313 us (86%)
  matrix products  23.5 us (6%)
  between operations  15 us (4%)
  local copies, waits for them, and re-layouts  9.38 us (3%)
    psum x1, waiting for transfers between devices, local(): gram = lax.psum(partial_gram, ('item', 'user'))  211 us
    all_gather x1, waiting for transfers between devices, local(): all_rows = lax.all_gather(item_factors, 'item', axis=0, tiled=True)  101 us
    dot_general x5, matrix products, apply_system(): jnp.einsum('bkui,bkir->bur', scores * weights, tiles, precision=HIGHEST)  9.1 us
  transfers between devices with their start and end apart: 2, of which 2 were waited for; matrix products, arithmetic and copies ran while one was open for 5% of the time, Pallas kernels for 0%

commit v1 on v0

v1 whole, which is shorter than its diff:
```python
import jax
import jax.numpy as jnp
from jax import lax
from jax.experimental import pallas as pl
from jax.experimental.pallas import tpu as pltpu
from jax.sharding import PartitionSpec as P

ITERS = 4
RIDGE_WEIGHT = 0.1
EPSILON = 1e-06
TILE = 128
NEAR = 8
SLICE = TILE // NEAR


def halves(x):
    high = x.astype(jnp.bfloat16)
    low = (x - high.astype(jnp.float32)).astype(jnp.bfloat16)
    return high, low


def quadrants(x):
    rows, cols = x.shape[0] // 2, x.shape[1] // 2
    return (x[:rows, :cols] + x[:rows, cols:]) + (x[rows:, :cols] + x[rows:, cols:])


def prep_kernel(place_ref, shard_ref, out_ref, gram_ref):
    start = pl.multiple_of(place_ref[0] * SLICE, SLICE)
    tiles = shard_ref.shape[0] // TILE
    high, low = halves(shard_ref[...])
    both = jnp.concatenate([high, low], axis=1)
    gram_ref[...] = quadrants(
        lax.dot_general(both, both, (((0,), (0,)), ((), ())), preferred_element_type=jnp.float32)
    )
    pieces = [shard_ref[pl.ds(t * TILE + start, SLICE), :] for t in range(tiles)]
    pieces.append(gram_ref[pl.ds(start, SLICE), :])
    for t, piece in enumerate(pieces):
        for d in range(out_ref.shape[0]):
            out_ref[d, t * SLICE:(t + 1) * SLICE, :] = piece


def pick_kernel(core_ref, lists_ref, mine_ref, other_ref, out_ref):
    near, slots = lists_ref.shape
    core = core_ref[0]
    held = mine_ref.shape[1] // SLICE - 1
    last = held * SLICE
    gram = mine_ref[0, last:, :] + other_ref[0, last:, :]
    for y in range(1, mine_ref.shape[0]):
        gram = gram + (mine_ref[y, last:, :] + other_ref[y, last:, :])

    def one(d, _):
        for k in range(slots):
            tile = lists_ref[d, k]
            shard = tile // held
            row = shard // 2
            at = pl.multiple_of((tile - shard * held) * SLICE, SLICE)
            same = (shard - row * 2) == core
            a = mine_ref[row, pl.ds(at, SLICE), :]
            b = other_ref[row, pl.ds(at, SLICE), :]
            out_ref[d, k * SLICE:(k + 1) * SLICE, :] = jnp.where(same, a, b)
        out_ref[d, slots * SLICE:, :] = gram
        return 0

    lax.fori_loop(0, near, one, 0)


def solve_kernel(tiles_ref, weights_ref, start_ref, out_ref, y_ref, resid_ref, dir_ref):
    near = tiles_ref.shape[0]
    slots = weights_ref.shape[0]
    items = slots * TILE
    chunk = 2 * TILE

    for k in range(slots + 1):
        for p in range(near):
            high, low = halves(tiles_ref[p, k * SLICE:(k + 1) * SLICE, :])
            at = k * TILE + p * SLICE
            y_ref[at:at + SLICE, :TILE] = high
            y_ref[at:at + SLICE, TILE:] = low

    def wide(n):
        return jnp.concatenate([weights_ref[2 * n], weights_ref[2 * n + 1]], axis=1)

    def apply(v):
        high, low = halves(v)
        left = jnp.concatenate(
            [jnp.concatenate([high, high], axis=1), jnp.concatenate([low, low], axis=1)], axis=0
        )
        total = None
        for n in range(items // chunk):
            rows = y_ref[n * chunk:(n + 1) * chunk, :]
            s = lax.dot_general(left, rows, (((1,), (1,)), ((), ())), preferred_element_type=jnp.float32)
            scores = (s[:TILE] + s[TILE:]) * wide(n).astype(jnp.float32)
            part = jnp.dot(
                jnp.concatenate(halves(scores), axis=0), rows, preferred_element_type=jnp.float32
            )
            total = part if total is None else total + part
        g = lax.dot_general(
            left, y_ref[items:, :], (((1,), (1,)), ((), ())), preferred_element_type=jnp.float32
        )
        return quadrants(total) + (g[:TILE] + g[TILE:]) + RIDGE_WEIGHT * v

    ones = jnp.ones((16, chunk), jnp.bfloat16)
    total = None
    for n in range(items // chunk):
        part = jnp.dot(
            jnp.concatenate([wide(n), ones], axis=0),
            y_ref[n * chunk:(n + 1) * chunk, :],
            preferred_element_type=jnp.float32,
        )
        total = part if total is None else total + part
    total = total[:, :TILE] + total[:, TILE:]
    target = total[:TILE] + total[TILE:TILE + 1]

    start = start_ref[...]
    resid = target - apply(start)
    out_ref[...] = start
    resid_ref[...] = resid
    dir_ref[...] = resid

    def step(_, norm_now):
        direction = dir_ref[...]
        image = apply(direction)
        alpha = norm_now / (jnp.sum(direction * image, axis=-1, keepdims=True) + EPSILON)
        out_ref[...] = out_ref[...] + alpha * direction
        resid = resid_ref[...] - alpha * image
        norm_next = jnp.sum(resid * resid, axis=-1, keepdims=True)
        resid_ref[...] = resid
        dir_ref[...] = resid + norm_next / (norm_now + EPSILON) * direction
        return norm_next

    lax.fori_loop(0, ITERS, step, jnp.sum(resid * resid, axis=-1, keepdims=True))


VMEM = pl.BlockSpec(memory_space=pltpu.VMEM)
SMEM = pl.BlockSpec(memory_space=pltpu.SMEM)


def local(item_factors, tile_lists, tile_weights, user_factors):
    rank = item_factors.shape[1]
    slots = tile_lists.shape[1]
    shards = lax.axis_size("item")
    users = lax.axis_size("user")
    rows_y = shards // 2
    column = [[2 * y + c for y in range(rows_y)] for c in range(2)]
    around = [[g * NEAR + j for j in range(NEAR)] for g in range(users // NEAR)]
    swap = [(i, i ^ 1) for i in range(shards)]
    place = (lax.axis_index("user") % NEAR).astype(jnp.int32).reshape(1)
    core = (lax.axis_index("item") % 2).astype(jnp.int32).reshape(1)
    held = item_factors.shape[0] // TILE

    send_a, _ = pl.pallas_call(
        prep_kernel,
        out_shape=(
            jax.ShapeDtypeStruct((rows_y, (held + 1) * SLICE, rank), jnp.float32),
            jax.ShapeDtypeStruct((rank, rank), jnp.float32),
        ),
        in_specs=[SMEM, VMEM],
        out_specs=(VMEM, VMEM),
        name="prep",
    )(place, item_factors)
    with jax.named_scope("column"):
        mine = lax.all_to_all(send_a, "item", 0, 0, tiled=True, axis_index_groups=column)
    with jax.named_scope("lists"):
        near_lists = lax.all_to_all(
            jnp.broadcast_to(tile_lists, (NEAR, slots)), "user", 0, 0, tiled=True, axis_index_groups=around
        )
    with jax.named_scope("swap"):
        other = lax.ppermute(mine, "item", swap)
    send_b = pl.pallas_call(
        pick_kernel,
        out_shape=jax.ShapeDtypeStruct((NEAR, (slots + 1) * SLICE, rank), jnp.float32),
        in_specs=[SMEM, SMEM, VMEM, VMEM],
        out_specs=VMEM,
        name="pick",
    )(core, near_lists, mine, other)
    with jax.named_scope("around"):
        tiles = lax.all_to_all(send_b, "user", 0, 0, tiled=True, axis_index_groups=around)
    return pl.pallas_call(
        solve_kernel,
        out_shape=jax.ShapeDtypeStruct((TILE, rank), jnp.float32),
        in_specs=[VMEM, VMEM, VMEM],
        out_specs=VMEM,
        scratch_shapes=[
            pltpu.VMEM(((slots + 1) * TILE, 2 * rank), jnp.bfloat16),
            pltpu.VMEM((TILE, rank), jnp.float32),
            pltpu.VMEM((TILE, rank), jnp.float32),
        ],
        name="solve",
    )(tiles, tile_weights[0], user_factors)


def solution(mesh):
    in_specs = (
        P("item", None),
        P(("item", "user"), None),
        P(("item", "user"), None, None, None),
        P(("item", "user"), None),
    )
    out_specs = P(("item", "user"), None)
    return jax.shard_map(local, mesh=mesh, in_specs=in_specs, out_specs=out_specs, check_vma=False)
```

time: 363 us -> 88 us (0.24)
  waiting for transfers between devices: 313 us -> 4.96 us
  blocking collectives: 0 us -> 53.7 us
  matrix products: 23.5 us -> 0 us
  between operations: 15 us -> 0.03 us
  Pallas kernels: 0 us -> 14.3 us
  starting transfers between devices: 0.05 us -> 11.8 us
  local copies, waits for them, and re-layouts: 9.38 us -> 1.59 us
    psum x1 -> x0, waiting for transfers between devices: 211 us -> none  [local(): gram = lax.psum(partial_gram, ('item', 'user'))]
    all_gather x1 -> x0, waiting for transfers between devices: 101 us -> none  [local(): all_rows = lax.all_gather(item_factors, 'item', axis=0, tiled=True)]
    all_to_all x0 -> x2, blocking collectives: none -> 53.7 us  [the longest x1 34.8 us: local(): lax.all_to_all(send_a, 'item', 0, 0, tiled=True, axis_index_groups=column)]
    dot_general x17 -> x0, matrix products: 23.5 us -> none  [the longest x5 9.1 us: apply_system(): jnp.einsum('bkui,bkir->bur', scores * weights, tiles, precision=HIGHEST)]
    pallas_call x0 -> x3, Pallas kernels: none -> 14.3 us  [the longest x1 7.35 us: local(): pl.pallas_call(solve_kernel, out_shape=jax.ShapeDtypeStruct((TILE, rank),...]
    gather x1 -> x0, local copies, waits for them, and re-layouts: 6.41 us -> none  [local(): fetched = all_rows.reshape(-1, tile_side, factor_rank)[tile_ids]]
    ppermute x0 -> x1, starting transfers between devices: none -> 5.96 us  [local(): other = lax.ppermute(mine, 'item', swap)]
    all_to_all x0 -> x1, starting transfers between devices: none -> 5.83 us  [local(): lax.all_to_all(jnp.broadcast_to(tile_lists, (NEAR, slots)), 'user', 0, 0,...]
  transfers between devices with their start and end apart: 2 -> 2, of which waited for: 2 -> 1; matrix products, arithmetic and copies ran while one was open for 5% -> 1% of each run, Pallas kernels for 0% -> 0%
where the time goes in v1:
time: 88 us; the launch traced here: 86.4 us
  blocking collectives  53.7 us (61%)
  Pallas kernels  14.3 us (16%)
  starting transfers between devices  11.8 us (13%)
  waiting for transfers between devices  4.96 us (6%)
  local copies, waits for them, and re-layouts  1.59 us (2%)
    all_to_all x1, blocking collectives, local(): lax.all_to_all(send_a, 'item', 0, 0, tiled=True, axis_index_groups=column)  34.8 us
    all_to_all x1, blocking collectives, local(): lax.all_to_all(send_b, 'user', 0, 0, tiled=True, axis_index_groups=around)  18.9 us
    pallas_call x1, Pallas kernels, local(): pl.pallas_call(solve_kernel, out_shape=jax.ShapeDtypeStruct((TILE, rank),...  7.35 us
    ppermute x1, starting transfers between devices, local(): other = lax.ppermute(mine, 'item', swap)  5.96 us
    all_to_all x1, starting transfers between devices, local(): lax.all_to_all(jnp.broadcast_to(tile_lists, (NEAR, slots)), 'user', 0, 0,...  5.83 us
    all_to_all x1, waiting for transfers between devices, local(): lax.all_to_all(jnp.broadcast_to(tile_lists, (NEAR, slots)), 'user', 0, 0,...  4.96 us
    pallas_call x1, Pallas kernels, local(): pl.pallas_call(pick_kernel, out_shape=jax.ShapeDtypeStruct((NEAR, (slots...  4.2 us
    pallas_call x1, Pallas kernels, local(): pl.pallas_call(prep_kernel, out_shape=(jax.ShapeDtypeStruct((rows_y, (hel...  2.72 us
  transfers between devices with their start and end apart: 2, of which 1 were waited for; matrix products, arithmetic and copies ran while one was open for 1% of the time, Pallas kernels for 0%

profile of v1, /device:TPU:1, one launch (start us, length us, event | category | flops | bytes accessed | tf_op | source)
XLA Modules:
  0.0 86.4 jit_solution(8682897131293164097)
XLA Ops:
  0.0 2.7 %prep.1 = (f32[8,272,128]{2,1,0:T(8,128)}, f32[128,128]{1,0:T(8,128)}) custom-call(s32[1]{0:T(128)} %bitcast.3.place_ref, f32[2048,128]{1,0:T(8,128)} %shard_ref.1), custom_call_target="tpu_custom_call" | custom-call | tf_op jit(solution)/shard_map/prep/pallas_call | solution.py:151
  2.7 0.0 copy-start.3
  2.7 34.8 %all_to_all.18.mine_ref = f32[8,272,128]{2,1,0:T(8,128)S(1)} all-to-all(f32[8,272,128]{2,1,0:T(8,128)} %get-tuple-element.6), channel_id=1, replica_groups={{0,64,128,192,256,320,384,448},{32,96,160,224,288,352,416,480},{1,65,12..., dimensions={0} | all-to-all | bytes 2228224 | tf_op jit(solution)/shard_map/column/all_to_all | solution.py:162
  37.5 0.0 copy-start
  37.5 6.0 %collective-permute-start = (f32[8,272,128]{2,1,0:T(8,128)S(1)}, f32[8,272,128]{2,1,0:T(8,128)S(1)}, u32[]{:S(2)}, u32[]{:S(2)}) collective-permute-start(f32[8,272,128]{2,1,0:T(8,128)S(1)} %all_to_all.18.mine_ref), channel_id=1, source_target_pairs={{0,32},{32,0},{64,96},{96,64},{128,160},{160,128},{192,224},{224,1... | collective-permute-start | bytes 3342344 | tf_op jit(solution)/shard_map/swap/ppermute | solution.py:168
  43.5 0.0 copy-done.3
  43.5 0.6 broadcast_in_dim.2
  44.1 5.8 %all-to-all-start = ((s32[8,1,16]{2,1,0:T(1,128)}), s32[8,1,16]{2,1,0:T(1,128)S(1)}, u32[]{:S(2)}, u32[]{:S(2)}) async-start(s32[8,1,16]{2,1,0:T(1,128)} %broadcast_in_dim.2), calls=%async_computation | async-start | bytes 8192 | tf_op jit(solution)/shard_map/lists/all_to_all | solution.py:164
  49.9 5.0 %all-to-all-done = s32[8,1,16]{2,1,0:T(1,128)S(1)} async-done(((s32[8,1,16]{2,1,0:T(1,128)}), s32[8,1,16]{2,1,0:T(1,128)S(1)}, u32[]{:S(2)}, u32[]{:S(2)}) %all-to-all-start) | async-done | bytes 544 | tf_op jit(solution)/shard_map/lists/all_to_all | solution.py:164
  54.9 0.0 copy-start.2
  54.9 0.0 collective-permute-done.other_ref
  54.9 0.0 copy-start.1
  54.9 0.0 copy-done
  54.9 0.6 copy-done.2
  55.5 0.4 copy-done.1
  55.9 4.2 %pick.1 = f32[8,272,128]{2,1,0:T(8,128)} custom-call(s32[1]{0:T(128)} %bitcast.core_ref, s32[8,16]{1,0:T(8,128)} %bitcast.6, f32[8,272,128]{2,1,0:T(8,128)} %copy-done, f32[8,272,128]{2,1,0:T(8,128)} %copy-done.1), custom_call_target="tpu_custom_call" | custom-call | tf_op jit(solution)/shard_map/pick/pallas_call | solution.py:169
  60.1 18.9 %all_to_all.19.tiles_ref = f32[8,272,128]{2,1,0:T(8,128)} all-to-all(f32[8,272,128]{2,1,0:T(8,128)} %pick.1), channel_id=1, replica_groups={{0,1,2,3,4,5,6,7},{8,9,10,11,12,13,14,15},{16,17,18,19,20,21,22,23},{24..., dimensions={0} | all-to-all | bytes 2228224 | tf_op jit(solution)/shard_map/around/all_to_all | solution.py:177
  79.0 7.3 %solve.1 = f32[128,128]{1,0:T(8,128)} custom-call(f32[8,272,128]{2,1,0:T(8,128)} %all_to_all.19.tiles_ref, bf16[16,128,128]{2,1,0:T(8,128)(2,1)} %bitcast.5, f32[128,128]{1,0:T(8,128)} %start_ref.1), custom_call_target="tpu_custom_call" | custom-call | tf_op jit(solution)/shard_map/solve/pallas_call | solution.py:178
Async XLA Ops:
  2.7 40.8 %copy-start.3 = (s32[1,16]{1,0:T(1,128)S(1)}, s32[1,16]{1,0:T(1,128)}, u32[]{:S(2)}) copy-start(s32[1,16]{1,0:T(1,128)} %param.5) | copy-start | bytes 196
  37.5 17.4 %copy-start = (f32[8,272,128]{2,1,0:T(8,128)}, f32[8,272,128]{2,1,0:T(8,128)S(1)}, u32[]{:S(2)}) copy-start(f32[8,272,128]{2,1,0:T(8,128)S(1)} %all_to_all.18.mine_ref) | copy-start | bytes 3342340
  37.5 17.4 %collective-permute-start = (f32[8,272,128]{2,1,0:T(8,128)S(1)}, f32[8,272,128]{2,1,0:T(8,128)S(1)}, u32[]{:S(2)}, u32[]{:S(2)}) collective-permute-start(f32[8,272,128]{2,1,0:T(8,128)S(1)} %all_to_all.18.mine_ref), channel_id=1, source_target_pairs={{0,32},{32,0},{64,96},{96,64},{128,160},{160,128},{192,224},{224,1... | collective-permute-start | bytes 3342344 | tf_op jit(solution)/shard_map/swap/ppermute | solution.py:168
  44.1 10.8 %all-to-all-start = ((s32[8,1,16]{2,1,0:T(1,128)}), s32[8,1,16]{2,1,0:T(1,128)S(1)}, u32[]{:S(2)}, u32[]{:S(2)}) async-start(s32[8,1,16]{2,1,0:T(1,128)} %broadcast_in_dim.2), calls=%async_computation | async-start | bytes 8192 | tf_op jit(solution)/shard_map/lists/all_to_all | solution.py:164
  54.9 0.6 copy-start.2
  54.9 1.0 %copy-start.1 = (f32[8,272,128]{2,1,0:T(8,128)}, f32[8,272,128]{2,1,0:T(8,128)S(1)}, u32[]{:S(2)}) copy-start(f32[8,272,128]{2,1,0:T(8,128)S(1)} %collective-permute-done.other_ref) | copy-start | bytes 3342340

commit v2 on v1

--- a/solution.py
+++ b/solution.py
@@ -4,6 +4,7 @@
 from jax.experimental import pallas as pl
 from jax.experimental.pallas import tpu as pltpu
 from jax.sharding import PartitionSpec as P
+
 
 ITERS = 4
 RIDGE_WEIGHT = 0.1
@@ -39,9 +40,9 @@
             out_ref[d, t * SLICE:(t + 1) * SLICE, :] = piece
 
 
-def pick_kernel(core_ref, lists_ref, mine_ref, other_ref, out_ref):
+def pick_kernel(core_ref, place_ref, lists_ref, mine_ref, other_ref, out_ref):
     near, slots = lists_ref.shape
-    core = core_ref[0]
+    core, place = core_ref[0], place_ref[0]
     held = mine_ref.shape[1] // SLICE - 1
     last = held * SLICE
     gram = mine_ref[0, last:, :] + other_ref[0, last:, :]
@@ -49,16 +50,16 @@
         gram = gram + (mine_ref[y, last:, :] + other_ref[y, last:, :])
 
     def one(d, _):
+        to = place ^ d
         for k in range(slots):
             tile = lists_ref[d, k]
-            shard = tile // held
-            row = shard // 2
-            at = pl.multiple_of((tile - shard * held) * SLICE, SLICE)
-            same = (shard - row * 2) == core
+            shard = tile >> (held.bit_length() - 1)
+            row = shard >> 1
+            at = pl.multiple_of((tile & (held - 1)) * SLICE, SLICE)
             a = mine_ref[row, pl.ds(at, SLICE), :]
             b = other_ref[row, pl.ds(at, SLICE), :]
-            out_ref[d, k * SLICE:(k + 1) * SLICE, :] = jnp.where(same, a, b)
-        out_ref[d, slots * SLICE:, :] = gram
+            out_ref[to, k * SLICE:(k + 1) * SLICE, :] = jnp.where((shard & 1) == core, a, b)
+        out_ref[to, slots * SLICE:, :] = gram
         return 0
 
     lax.fori_loop(0, near, one, 0)
@@ -135,7 +136,11 @@
 SMEM = pl.BlockSpec(memory_space=pltpu.SMEM)
 
 
-def local(item_factors, tile_lists, tile_weights, user_factors):
+def grant(mib):
+    return pltpu.CompilerParams(vmem_limit_bytes=mib << 20)
+
+
+def chain(item_factors, tile_lists, tile_weights, user_factors):
     rank = item_factors.shape[1]
     slots = tile_lists.shape[1]
     shards = lax.axis_size("item")
@@ -148,33 +153,30 @@
     core = (lax.axis_index("item") % 2).astype(jnp.int32).reshape(1)
     held = item_factors.shape[0] // TILE
 
-    send_a, _ = pl.pallas_call(
+    send_a = pl.pallas_call(
         prep_kernel,
-        out_shape=(
-            jax.ShapeDtypeStruct((rows_y, (held + 1) * SLICE, rank), jnp.float32),
-            jax.ShapeDtypeStruct((rank, rank), jnp.float32),
-        ),
+        out_shape=jax.ShapeDtypeStruct((rows_y, (held + 1) * SLICE, rank), jnp.float32),
         in_specs=[SMEM, VMEM],
-        out_specs=(VMEM, VMEM),
+        out_specs=VMEM,
+        scratch_shapes=[pltpu.VMEM((rank, rank), jnp.float32)],
+        compiler_params=grant(16),
         name="prep",
     )(place, item_factors)
-    with jax.named_scope("column"):
-        mine = lax.all_to_all(send_a, "item", 0, 0, tiled=True, axis_index_groups=column)
-    with jax.named_scope("lists"):
-        near_lists = lax.all_to_all(
-            jnp.broadcast_to(tile_lists, (NEAR, slots)), "user", 0, 0, tiled=True, axis_index_groups=around
-        )
-    with jax.named_scope("swap"):
-        other = lax.ppermute(mine, "item", swap)
+    mine = lax.all_to_all(send_a, "item", 0, 0, tiled=True, axis_index_groups=column)
+    near_lists = tile_lists
+    for bit in (1, 2, 4):
+        step = [(u, u ^ bit) for u in range(users)]
+        near_lists = jnp.concatenate([near_lists, lax.ppermute(near_lists, "user", step)], axis=0)
+    other = lax.ppermute(mine, "item", swap)
     send_b = pl.pallas_call(
         pick_kernel,
         out_shape=jax.ShapeDtypeStruct((NEAR, (slots + 1) * SLICE, rank), jnp.float32),
-        in_specs=[SMEM, SMEM, VMEM, VMEM],
+        in_specs=[SMEM, SMEM, SMEM, VMEM, VMEM],
         out_specs=VMEM,
+        compiler_params=grant(12),
         name="pick",
-    )(core, near_lists, mine, other)
-    with jax.named_scope("around"):
-        tiles = lax.all_to_all(send_b, "user", 0, 0, tiled=True, axis_index_groups=around)
+    )(core, place, near_lists, mine, other)
+    tiles = lax.all_to_all(send_b, "user", 0, 0, tiled=True, axis_index_groups=around)
     return pl.pallas_call(
         solve_kernel,
         out_shape=jax.ShapeDtypeStruct((TILE, rank), jnp.float32),
@@ -185,6 +187,7 @@
             pltpu.VMEM((TILE, rank), jnp.float32),
             pltpu.VMEM((TILE, rank), jnp.float32),
         ],
+        compiler_params=grant(24),
         name="solve",
     )(tiles, tile_weights[0], user_factors)
 
@@ -197,4 +200,4 @@
         P(("item", "user"), None),
     )
     out_specs = P(("item", "user"), None)
-    return jax.shard_map(local, mesh=mesh, in_specs=in_specs, out_specs=out_specs, check_vma=False)
+    return jax.shard_map(chain, mesh=mesh, in_specs=in_specs, out_specs=out_specs, check_vma=False)

time: 88 us -> 85.9 us (0.976)
  the two profiles are of different devices: /device:TPU:1 before, /device:TPU:128 now
where the time goes in v2:
time: 85.9 us; the launch traced here: 85.6 us
  blocking collectives  56.5 us (66%)
  starting transfers between devices  14.5 us (17%)
  Pallas kernels  7.57 us (9%)
  waiting for transfers between devices  5.62 us (7%)
  local copies, waits for them, and re-layouts  1.24 us (1%)
    all_to_all x1, blocking collectives, chain(): lax.all_to_all(send_a, 'item', 0, 0, tiled=True, axis_index_groups=column)  37 us
    all_to_all x1, blocking collectives, chain(): lax.all_to_all(send_b, 'user', 0, 0, tiled=True, axis_index_groups=around)  19.5 us
    ppermute x3, starting transfers between devices, chain(): lax.ppermute(near_lists, 'user', step)  12.6 us
    pallas_call x1, Pallas kernels, chain(): pl.pallas_call(solve_kernel, out_shape=jax.ShapeDtypeStruct((TILE, rank),...  5.93 us
    ppermute x3, waiting for transfers between devices, chain(): lax.ppermute(near_lists, 'user', step)  5.62 us
    ppermute x1, starting transfers between devices, chain(): other = lax.ppermute(mine, 'item', swap)  1.91 us
  transfers between devices with their start and end apart: 4, of which 3 were waited for; matrix products, arithmetic and copies ran while one was open for 0% of the time, Pallas kernels for 0%

profile of v2, /device:TPU:128, one launch (start us, length us, event | category | flops | bytes accessed | tf_op | source)
XLA Modules:
  0.0 85.6 jit_solution(7709531200981366870)
XLA Ops:
  0.0 0.0 copy-start
  0.0 1.2 %copy-done = f32[2048,128]{1,0:T(8,128)S(1)} copy-done((f32[2048,128]{1,0:T(8,128)S(1)}, f32[2048,128]{1,0:T(8,128)}, u32[]{:S(2)}) %copy-start) | copy-done | bytes 1048600
  1.2 0.5 prep.1
  1.7 0.0 copy-start.3
  1.7 37.0 %all_to_all.10.mine_ref = f32[8,272,128]{2,1,0:T(8,128)S(1)} all-to-all(f32[8,272,128]{2,1,0:T(8,128)S(1)} %prep.1), channel_id=1, replica_groups={{0,64,128,192,256,320,384,448},{32,96,160,224,288,352,416,480},{1,65,12..., dimensions={0} | all-to-all | bytes 2228224 | tf_op jit(solution)/shard_map/all_to_all | solution.py:165
  38.8 1.9 %collective-permute-start.3 = (f32[8,272,128]{2,1,0:T(8,128)S(1)}, f32[8,272,128]{2,1,0:T(8,128)S(1)}, u32[]{:S(2)}, u32[]{:S(2)}) collective-permute-start(f32[8,272,128]{2,1,0:T(8,128)S(1)} %all_to_all.10.mine_ref), channel_id=1, source_target_pairs={{0,32},{32,0},{64,96},{96,64},{128,160},{160,128},{192,224},{224,1... | collective-permute-start | bytes 3342344 | tf_op jit(solution)/shard_map/ppermute | solution.py:170
  40.7 0.0 copy-done.3
  40.7 3.4 %collective-permute-start = (s32[1,16]{1,0:T(1,128)S(1)}, s32[1,16]{1,0:T(1,128)S(1)}, u32[]{:S(2)}, u32[]{:S(2)}) collective-permute-start(s32[1,16]{1,0:T(1,128)S(1)} %copy-done.3), channel_id=1, source_target_pairs={{0,1},{1,0},{2,3},{3,2},{4,5},{5,4},{6,7},{7,6},{8,9},{9,8},{10,11... | collective-permute-start | bytes 200 | tf_op jit(solution)/shard_map/ppermute | solution.py:169
  44.1 2.0 %collective-permute-done = s32[1,16]{1,0:T(1,128)S(1)} collective-permute-done((s32[1,16]{1,0:T(1,128)S(1)}, s32[1,16]{1,0:T(1,128)S(1)}, u32[]{:S(2)}, u32[]{:S(2)}) %collective-permute-start) | collective-permute-done | bytes 96 | tf_op jit(solution)/shard_map/ppermute | solution.py:169
  46.2 4.9 %collective-permute-start.1 = (s32[2,16]{1,0:T(2,128)S(1)}, s32[2,16]{1,0:T(2,128)S(1)}, u32[]{:S(2)}, u32[]{:S(2)}) collective-permute-start(s32[2,16]{1,0:T(2,128)S(1)} %pad_add_fusion.2), channel_id=1, source_target_pairs={{0,2},{1,3},{2,0},{3,1},{4,6},{5,7},{6,4},{7,5},{8,10},{9,11},{10,... | collective-permute-start | bytes 392 | tf_op jit(solution)/shard_map/ppermute | solution.py:169
  51.1 2.0 %collective-permute-done.1 = s32[2,16]{1,0:T(2,128)S(1)} collective-permute-done((s32[2,16]{1,0:T(2,128)S(1)}, s32[2,16]{1,0:T(2,128)S(1)}, u32[]{:S(2)}, u32[]{:S(2)}) %collective-permute-start.1) | collective-permute-done | bytes 160 | tf_op jit(solution)/shard_map/ppermute | solution.py:169
  53.1 4.3 %collective-permute-start.2 = (s32[4,16]{1,0:T(4,128)S(1)}, s32[4,16]{1,0:T(4,128)S(1)}, u32[]{:S(2)}, u32[]{:S(2)}) collective-permute-start(s32[4,16]{1,0:T(4,128)S(1)} %pad_add_fusion.1), channel_id=1, source_target_pairs={{0,4},{1,5},{2,6},{3,7},{4,0},{5,1},{6,2},{7,3},{8,12},{9,13},{10,... | collective-permute-start | bytes 776 | tf_op jit(solution)/shard_map/ppermute | solution.py:169
  57.4 1.5 %collective-permute-done.2 = s32[4,16]{1,0:T(4,128)S(1)} collective-permute-done((s32[4,16]{1,0:T(4,128)S(1)}, s32[4,16]{1,0:T(4,128)S(1)}, u32[]{:S(2)}, u32[]{:S(2)}) %collective-permute-start.2) | collective-permute-done | bytes 288 | tf_op jit(solution)/shard_map/ppermute | solution.py:169
  59.0 0.0 collective-permute-done.3.other_ref
  59.0 1.1 %pick.1 = f32[8,272,128]{2,1,0:T(8,128)S(1)} custom-call(s32[1]{0:T(128)} %bitcast.core_ref, s32[1]{0:T(128)} %bitcast.1.place_ref, s32[8,16]{1,0:T(8,128)S(1)} %pad_add_fusion.lists_ref, f32[8,272,128]{2,1,0:T(8,128)S(1)} %all_to_all.10.mine_ref, f32[8,272,128]{2,1,0:T(8,128)S(1)} %collective-permute-done.3.other_ref), custom_call_target="tpu_custom_call" | custom-call | tf_op jit(solution)/shard_map/pick/pallas_call | solution.py:171
  60.2 0.0 copy-start.1
  60.2 0.0 copy-start.2
  60.2 19.5 %all_to_all.11.tiles_ref = f32[8,272,128]{2,1,0:T(8,128)S(1)} all-to-all(f32[8,272,128]{2,1,0:T(8,128)S(1)} %pick.1), channel_id=1, replica_groups={{0,1,2,3,4,5,6,7},{8,9,10,11,12,13,14,15},{16,17,18,19,20,21,22,23},{24..., dimensions={0} | all-to-all | bytes 2228224 | tf_op jit(solution)/shard_map/all_to_all | solution.py:179
  79.6 0.0 copy-done.1
  79.6 0.0 copy-done.2
  79.7 5.9 %solve.1 = f32[128,128]{1,0:T(8,128)} custom-call(f32[8,272,128]{2,1,0:T(8,128)S(1)} %all_to_all.11.tiles_ref, bf16[16,128,128]{2,1,0:T(8,128)(2,1)S(1)} %bitcast.3, f32[128,128]{1,0:T(8,128)S(1)} %copy-done.2), custom_call_target="tpu_custom_call" | custom-call | tf_op jit(solution)/shard_map/solve/pallas_call | solution.py:180
  (3 shorter events, 0.0 us)
Async XLA Ops:
  0.0 1.2 %copy-start = (f32[2048,128]{1,0:T(8,128)S(1)}, f32[2048,128]{1,0:T(8,128)}, u32[]{:S(2)}) copy-start(f32[2048,128]{1,0:T(8,128)} %shard_ref.1) | copy-start | bytes 3145732
  1.7 39.0 %copy-start.3 = (s32[1,16]{1,0:T(1,128)S(1)}, s32[1,16]{1,0:T(1,128)}, u32[]{:S(2)}) copy-start(s32[1,16]{1,0:T(1,128)} %param.5) | copy-start | bytes 196
  38.8 20.2 %collective-permute-start.3 = (f32[8,272,128]{2,1,0:T(8,128)S(1)}, f32[8,272,128]{2,1,0:T(8,128)S(1)}, u32[]{:S(2)}, u32[]{:S(2)}) collective-permute-start(f32[8,272,128]{2,1,0:T(8,128)S(1)} %all_to_all.10.mine_ref), channel_id=1, source_target_pairs={{0,32},{32,0},{64,96},{96,64},{128,160},{160,128},{192,224},{224,1... | collective-permute-start | bytes 3342344 | tf_op jit(solution)/shard_map/ppermute | solution.py:170
  40.7 5.5 %collective-permute-start = (s32[1,16]{1,0:T(1,128)S(1)}, s32[1,16]{1,0:T(1,128)S(1)}, u32[]{:S(2)}, u32[]{:S(2)}) collective-permute-start(s32[1,16]{1,0:T(1,128)S(1)} %copy-done.3), channel_id=1, source_target_pairs={{0,1},{1,0},{2,3},{3,2},{4,5},{5,4},{6,7},{7,6},{8,9},{9,8},{10,11... | collective-permute-start | bytes 200 | tf_op jit(solution)/shard_map/ppermute | solution.py:169
  46.2 7.0 %collective-permute-start.1 = (s32[2,16]{1,0:T(2,128)S(1)}, s32[2,16]{1,0:T(2,128)S(1)}, u32[]{:S(2)}, u32[]{:S(2)}) collective-permute-start(s32[2,16]{1,0:T(2,128)S(1)} %pad_add_fusion.2), channel_id=1, source_target_pairs={{0,2},{1,3},{2,0},{3,1},{4,6},{5,7},{6,4},{7,5},{8,10},{9,11},{10,... | collective-permute-start | bytes 392 | tf_op jit(solution)/shard_map/ppermute | solution.py:169
  53.1 5.8 %collective-permute-start.2 = (s32[4,16]{1,0:T(4,128)S(1)}, s32[4,16]{1,0:T(4,128)S(1)}, u32[]{:S(2)}, u32[]{:S(2)}) collective-permute-start(s32[4,16]{1,0:T(4,128)S(1)} %pad_add_fusion.1), channel_id=1, source_target_pairs={{0,4},{1,5},{2,6},{3,7},{4,0},{5,1},{6,2},{7,3},{8,12},{9,13},{10,... | collective-permute-start | bytes 776 | tf_op jit(solution)/shard_map/ppermute | solution.py:169
  60.2 19.5 %copy-start.1 = (bf16[1,16,128,128]{3,2,1,0:T(8,128)(2,1)S(1)}, bf16[1,16,128,128]{3,2,1,0:T(8,128)(2,1)}, u32[]{:S(2)}) copy-start(bf16[1,16,128,128]{3,2,1,0:T(8,128)(2,1)} %param.6) | copy-start | bytes 1572868
  60.2 19.5 %copy-start.2 = (f32[128,128]{1,0:T(8,128)S(1)}, f32[128,128]{1,0:T(8,128)}, u32[]{:S(2)}) copy-start(f32[128,128]{1,0:T(8,128)} %start_ref.1) | copy-start | bytes 196612

commit v3 on v2

v3 whole, which is shorter than its diff:
```python
import jax
import jax.numpy as jnp
from jax import lax
from jax.experimental import pallas as pl
from jax.experimental.pallas import tpu as pltpu
from jax.sharding import PartitionSpec as P


ITERS = 4
RIDGE_WEIGHT = 0.1
EPSILON = 1e-06
TILE = 128
NEAR = 8
SLICE = TILE // NEAR
ROWS = 8
PIECES = 2


def halves(x):
    high = x.astype(jnp.bfloat16)
    low = (x - high.astype(jnp.float32)).astype(jnp.bfloat16)
    return high, low


def quadrants(x):
    rows, cols = x.shape[0] // 2, x.shape[1] // 2
    return (x[:rows, :cols] + x[:rows, cols:]) + (x[rows:, :cols] + x[rows:, cols:])


def prep_kernel(place_ref, shard_ref, out_ref, held_ref, stage_ref, gram_ref, load_sems, slice_sem, out_sem):
    start = pl.multiple_of(place_ref[0] * SLICE, SLICE)
    rows = shard_ref.shape[0]
    tiles = rows // TILE
    part = rows // PIECES
    body, tail = pl.ds(0, tiles * SLICE), pl.ds(tiles * SLICE, SLICE)

    def load(p):
        at = pl.ds(p * part, part)
        return pltpu.make_async_copy(shard_ref.at[at], held_ref.at[at], load_sems.at[p])

    for t in range(tiles):
        pltpu.make_async_copy(
            shard_ref.at[pl.ds(t * TILE + start, SLICE)], stage_ref.at[pl.ds(t * SLICE, SLICE)], slice_sem
        ).start()
    for p in range(PIECES):
        load(p).start()
    pltpu.make_async_copy(shard_ref.at[body], stage_ref.at[body], slice_sem).wait()
    for d in range(out_ref.shape[0]):
        pltpu.make_async_copy(stage_ref.at[body], out_ref.at[d, body], out_sem).start()
    gram = None
    for p in range(PIECES):
        load(p).wait()
        both = jnp.concatenate(halves(held_ref[p * part:(p + 1) * part, :]), axis=1)
        more = lax.dot_general(
            both, both, (((0,), (0,)), ((), ())), preferred_element_type=jnp.float32
        )
        gram = more if gram is None else gram + more
    gram_ref[...] = quadrants(gram)
    stage_ref[tail, :] = gram_ref[pl.ds(start, SLICE), :]
    for d in range(out_ref.shape[0]):
        pltpu.make_async_copy(stage_ref.at[tail], out_ref.at[d, tail], out_sem).start()
    pltpu.make_async_copy(out_ref, out_ref, out_sem).wait()


def pick_kernel(place_ref, at_ref, same_ref, mine_ref, other_ref, out_ref):
    near, slots = at_ref.shape
    place = place_ref[0]
    step = (mine_ref.shape[0] // ROWS) - SLICE
    gram = None
    for y in range(ROWS):
        at = pl.ds(y * (step + SLICE) + step, SLICE)
        more = mine_ref[at, :] + other_ref[at, :]
        gram = more if gram is None else gram + more

    def one(d, _):
        to = place ^ d
        for k in range(slots):
            at = pl.ds(pl.multiple_of(at_ref[d, k], SLICE), SLICE)
            a, b = mine_ref[at, :], other_ref[at, :]
            out_ref[to, k * SLICE:(k + 1) * SLICE, :] = jnp.where(same_ref[d, k] != 0, a, b)
        out_ref[to, slots * SLICE:, :] = gram
        return 0

    lax.fori_loop(0, near, one, 0)


def solve_kernel(tiles_ref, weights_ref, start_ref, out_ref, y_ref, resid_ref, dir_ref):
    near = tiles_ref.shape[0]
    slots = weights_ref.shape[0]
    items = slots * TILE
    chunk = 2 * TILE

    for k in range(slots + 1):
        for p in range(near):
            high, low = halves(tiles_ref[p, k * SLICE:(k + 1) * SLICE, :])
            at = k * TILE + p * SLICE
            y_ref[at:at + SLICE, :TILE] = high
            y_ref[at:at + SLICE, TILE:] = low

    def wide(n):
        pair = jnp.concatenate([weights_ref[2 * n], weights_ref[2 * n + 1]], axis=1)
        return pair.astype(jnp.float32)

    def stacked(v):
        high, low = halves(v)
        return jnp.concatenate(
            [jnp.concatenate([high, high], axis=1), jnp.concatenate([low, low], axis=1)], axis=0
        )

    def scores(left, n):
        s = lax.dot_general(
            left, y_ref[n * chunk:(n + 1) * chunk, :], (((1,), (1,)), ((), ())),
            preferred_element_type=jnp.float32,
        )
        return s[:TILE] + s[TILE:]

    def ridge(left, v):
        g = lax.dot_general(
            left, y_ref[items:, :], (((1,), (1,)), ((), ())), preferred_element_type=jnp.float32
        )
        return (g[:TILE] + g[TILE:]) + RIDGE_WEIGHT * v

    def gathered(left, of):
        total = None
        for n in range(items // chunk):
            part = jnp.dot(
                jnp.concatenate(halves(of(scores(left, n), wide(n))), axis=0),
                y_ref[n * chunk:(n + 1) * chunk, :],
                preferred_element_type=jnp.float32,
            )
            total = part if total is None else total + part
        return quadrants(total)

    start = start_ref[...]
    left = stacked(start)
    resid = gathered(left, lambda s, w: 1.0 + w * (1.0 - s)) - ridge(left, start)
    out_ref[...] = start
    resid_ref[...] = resid
    dir_ref[...] = resid

    def step(_, norm_now):
        direction = dir_ref[...]
        left = stacked(direction)
        image = gathered(left, lambda s, w: s * w) + ridge(left, direction)
        alpha = norm_now / (jnp.sum(direction * image, axis=-1, keepdims=True) + EPSILON)
        out_ref[...] = out_ref[...] + alpha * direction
        resid = resid_ref[...] - alpha * image
        norm_next = jnp.sum(resid * resid, axis=-1, keepdims=True)
        resid_ref[...] = resid
        dir_ref[...] = resid + norm_next / (norm_now + EPSILON) * direction
        return norm_next

    norm = lax.fori_loop(0, ITERS - 1, step, jnp.sum(resid * resid, axis=-1, keepdims=True))
    direction = dir_ref[...]
    left = stacked(direction)
    total = None
    for n in range(items // chunk):
        s = scores(left, n)
        part = s * s * wide(n)
        total = part if total is None else total + part
    curve = total[:, :TILE] + total[:, TILE:] + direction * ridge(left, direction)
    alpha = norm / (jnp.sum(curve, axis=-1, keepdims=True) + EPSILON)
    out_ref[...] = out_ref[...] + alpha * direction


VMEM = pl.BlockSpec(memory_space=pltpu.VMEM)
SMEM = pl.BlockSpec(memory_space=pltpu.SMEM)


def grant(mib):
    return pltpu.CompilerParams(vmem_limit_bytes=mib << 20)


def chain(item_factors, tile_lists, tile_weights, user_factors):
    rank = item_factors.shape[1]
    slots = tile_lists.shape[1]
    shards = lax.axis_size("item")
    users = lax.axis_size("user")
    rows_y = shards // 2
    assert rows_y == ROWS
    column = [[2 * y + c for y in range(rows_y)] for c in range(2)]
    around = [[g * NEAR + j for j in range(NEAR)] for g in range(users // NEAR)]
    swap = [(i, i ^ 1) for i in range(shards)]
    place = (lax.axis_index("user") % NEAR).astype(jnp.int32).reshape(1)
    core = (lax.axis_index("item") % 2).astype(jnp.int32).reshape(1)
    held = item_factors.shape[0] // TILE

    send_a = pl.pallas_call(
        prep_kernel,
        out_shape=jax.ShapeDtypeStruct((rows_y, (held + 1) * SLICE, rank), jnp.float32),
        in_specs=[SMEM, pl.BlockSpec(memory_space=pltpu.MemorySpace.HBM)],
        out_specs=pl.BlockSpec(memory_space=pltpu.MemorySpace.HBM),
        scratch_shapes=[
            pltpu.VMEM(item_factors.shape, jnp.float32),
            pltpu.VMEM(((held + 1) * SLICE, rank), jnp.float32),
            pltpu.VMEM((rank, rank), jnp.float32),
            pltpu.SemaphoreType.DMA((PIECES,)),
            pltpu.SemaphoreType.DMA,
            pltpu.SemaphoreType.DMA,
        ],
        name="prep",
    )(place, item_factors)
    mine = lax.all_to_all(send_a, "item", 0, 0, tiled=True, axis_index_groups=column)
    near_lists = tile_lists
    for bit in (1, 2, 4):
        step = [(u, u ^ bit) for u in range(users)]
        near_lists = jnp.concatenate([near_lists, lax.ppermute(near_lists, "user", step)], axis=0)
    shard = near_lists // held
    at = ((shard // 2) * (held + 1) + near_lists % held) * SLICE
    same = (shard % 2 == core).astype(jnp.int32)
    other = lax.ppermute(mine, "item", swap)
    send_b = pl.pallas_call(
        pick_kernel,
        out_shape=jax.ShapeDtypeStruct((NEAR, (slots + 1) * SLICE, rank), jnp.float32),
        in_specs=[SMEM, SMEM, SMEM, VMEM, VMEM],
        out_specs=VMEM,
        compiler_params=grant(12),
        name="pick",
    )(place, at, same, mine.reshape(-1, rank), other.reshape(-1, rank))
    tiles = lax.all_to_all(send_b, "user", 0, 0, tiled=True, axis_index_groups=around)
    return pl.pallas_call(
        solve_kernel,
        out_shape=jax.ShapeDtypeStruct((TILE, rank), jnp.float32),
        in_specs=[VMEM, VMEM, VMEM],
        out_specs=VMEM,
        scratch_shapes=[
            pltpu.VMEM(((slots + 1) * TILE, 2 * rank), jnp.bfloat16),
            pltpu.VMEM((TILE, rank), jnp.float32),
            pltpu.VMEM((TILE, rank), jnp.float32),
        ],
        compiler_params=grant(24),
        name="solve",
    )(tiles, tile_weights[0], user_factors)


def solution(mesh):
    in_specs = (
        P("item", None),
        P(("item", "user"), None),
        P(("item", "user"), None, None, None),
        P(("item", "user"), None),
    )
    out_specs = P(("item", "user"), None)
    return jax.shard_map(chain, mesh=mesh, in_specs=in_specs, out_specs=out_specs, check_vma=False)
```

time: 85.9 us -> 86.2 us (level)
  Pallas kernels: 7.57 us -> 8.82 us
  local copies, waits for them, and re-layouts: 1.24 us -> 0.02 us
    pallas_call x1, Pallas kernels: 0.49 us -> 2.51 us  [chain(): pl.pallas_call(prep_kernel, out_shape=jax.ShapeDtypeStruct((rows_y, (held...]
    unnamed x8 -> x6, local copies, waits for them, and re-layouts: 1.24 us -> 0.02 us
where the time goes in v3:
time: 86.2 us; the launch traced here: 85.9 us
  blocking collectives  56.7 us (66%)
  starting transfers between devices  14.5 us (17%)
  Pallas kernels  8.82 us (10%)
  waiting for transfers between devices  5.63 us (7%)
    all_to_all x1, blocking collectives, chain(): lax.all_to_all(send_a, 'item', 0, 0, tiled=True, axis_index_groups=column)  37.2 us
    all_to_all x1, blocking collectives, chain(): lax.all_to_all(send_b, 'user', 0, 0, tiled=True, axis_index_groups=around)  19.5 us
    ppermute x3, starting transfers between devices, chain(): lax.ppermute(near_lists, 'user', step)  12.6 us
    ppermute x3, waiting for transfers between devices, chain(): lax.ppermute(near_lists, 'user', step)  5.63 us
    pallas_call x1, Pallas kernels, chain(): pl.pallas_call(solve_kernel, out_shape=jax.ShapeDtypeStruct((TILE, rank),...  5.32 us
    pallas_call x1, Pallas kernels, chain(): pl.pallas_call(prep_kernel, out_shape=jax.ShapeDtypeStruct((rows_y, (held...  2.51 us
    ppermute x1, starting transfers between devices, chain(): other = lax.ppermute(mine, 'item', swap)  1.91 us
  transfers between devices with their start and end apart: 4, of which 3 were waited for; matrix products, arithmetic and copies ran while one was open for 0% of the time, Pallas kernels for 0%

profile of v3, /device:TPU:128, one launch (start us, length us, event | category | flops | bytes accessed | tf_op | source)
XLA Modules:
  0.0 85.9 jit_solution(3437631367545154506)
XLA Ops:
  0.0 2.5 %prep.1 = f32[8,272,128]{2,1,0:T(8,128)} custom-call(s32[1]{0:T(128)} %bitcast.place_ref, f32[2048,128]{1,0:T(8,128)} %shard_ref.1), custom_call_target="tpu_custom_call" | custom-call | tf_op jit(solution)/shard_map/prep/pallas_call | solution.py:188
  2.5 0.0 copy-start.2
  2.5 37.2 %all_to_all.10 = f32[8,272,128]{2,1,0:T(8,128)S(1)} all-to-all(f32[8,272,128]{2,1,0:T(8,128)} %prep.1), channel_id=1, replica_groups={{0,64,128,192,256,320,384,448},{32,96,160,224,288,352,416,480},{1,65,12..., dimensions={0} | all-to-all | bytes 2228224 | tf_op jit(solution)/shard_map/all_to_all | solution.py:203
  39.8 1.9 %collective-permute-start.3 = (f32[8,272,128]{2,1,0:T(8,128)S(1)}, f32[8,272,128]{2,1,0:T(8,128)S(1)}, u32[]{:S(2)}, u32[]{:S(2)}) collective-permute-start(f32[8,272,128]{2,1,0:T(8,128)S(1)} %all_to_all.10), channel_id=1, source_target_pairs={{0,32},{32,0},{64,96},{96,64},{128,160},{160,128},{192,224},{224,1... | collective-permute-start | bytes 3342344 | tf_op jit(solution)/shard_map/ppermute | solution.py:211
  41.7 0.0 copy-done.2
  41.7 3.4 %collective-permute-start = (s32[1,16]{1,0:T(1,128)S(1)}, s32[1,16]{1,0:T(1,128)S(1)}, u32[]{:S(2)}, u32[]{:S(2)}) collective-permute-start(s32[1,16]{1,0:T(1,128)S(1)} %copy-done.2), channel_id=1, source_target_pairs={{0,1},{1,0},{2,3},{3,2},{4,5},{5,4},{6,7},{7,6},{8,9},{9,8},{10,11... | collective-permute-start | bytes 200 | tf_op jit(solution)/shard_map/ppermute | solution.py:207
  45.1 2.1 %collective-permute-done = s32[1,16]{1,0:T(1,128)S(1)} collective-permute-done((s32[1,16]{1,0:T(1,128)S(1)}, s32[1,16]{1,0:T(1,128)S(1)}, u32[]{:S(2)}, u32[]{:S(2)}) %collective-permute-start) | collective-permute-done | bytes 96 | tf_op jit(solution)/shard_map/ppermute | solution.py:207
  47.2 4.9 %collective-permute-start.1 = (s32[2,16]{1,0:T(2,128)S(1)}, s32[2,16]{1,0:T(2,128)S(1)}, u32[]{:S(2)}, u32[]{:S(2)}) collective-permute-start(s32[2,16]{1,0:T(2,128)S(1)} %pad_add_fusion.2), channel_id=1, source_target_pairs={{0,2},{1,3},{2,0},{3,1},{4,6},{5,7},{6,4},{7,5},{8,10},{9,11},{10,... | collective-permute-start | bytes 392 | tf_op jit(solution)/shard_map/ppermute | solution.py:207
  52.1 2.0 %collective-permute-done.1 = s32[2,16]{1,0:T(2,128)S(1)} collective-permute-done((s32[2,16]{1,0:T(2,128)S(1)}, s32[2,16]{1,0:T(2,128)S(1)}, u32[]{:S(2)}, u32[]{:S(2)}) %collective-permute-start.1) | collective-permute-done | bytes 160 | tf_op jit(solution)/shard_map/ppermute | solution.py:207
  54.1 4.3 %collective-permute-start.2 = (s32[4,16]{1,0:T(4,128)S(1)}, s32[4,16]{1,0:T(4,128)S(1)}, u32[]{:S(2)}, u32[]{:S(2)}) collective-permute-start(s32[4,16]{1,0:T(4,128)S(1)} %pad_add_fusion.1), channel_id=1, source_target_pairs={{0,4},{1,5},{2,6},{3,7},{4,0},{5,1},{6,2},{7,3},{8,12},{9,13},{10,... | collective-permute-start | bytes 776 | tf_op jit(solution)/shard_map/ppermute | solution.py:207
  58.4 1.5 %collective-permute-done.2 = s32[4,16]{1,0:T(4,128)S(1)} collective-permute-done((s32[4,16]{1,0:T(4,128)S(1)}, s32[4,16]{1,0:T(4,128)S(1)}, u32[]{:S(2)}, u32[]{:S(2)}) %collective-permute-start.2) | collective-permute-done | bytes 288 | tf_op jit(solution)/shard_map/ppermute | solution.py:207
  60.0 0.0 collective-permute-done.3
  60.1 1.0 %pick.1 = f32[8,272,128]{2,1,0:T(8,128)S(1)} custom-call(s32[1]{0:T(128)} %bitcast.place_ref, s32[8,16]{1,0:T(8,128)S(1)} %fusion.2.at_ref, s32[8,16]{1,0:T(8,128)S(1)} %fusion.6.same_ref, f32[2176,128]{1,0:T(8,128)S(1)} %bitcast.4, f32[2176,128]{1,0:T(8,128)S(1)} %bitcast.5), custom_call_target="tpu_custom_call" | custom-call | tf_op jit(solution)/shard_map/pick/pallas_call | solution.py:212
  61.0 0.0 copy-start
  61.1 0.0 copy-start.1
  61.1 19.5 %all_to_all.11.tiles_ref = f32[8,272,128]{2,1,0:T(8,128)S(1)} all-to-all(f32[8,272,128]{2,1,0:T(8,128)S(1)} %pick.1), channel_id=1, replica_groups={{0,1,2,3,4,5,6,7},{8,9,10,11,12,13,14,15},{16,17,18,19,20,21,22,23},{24..., dimensions={0} | all-to-all | bytes 2228224 | tf_op jit(solution)/shard_map/all_to_all | solution.py:220
  80.5 0.0 copy-done
  80.5 0.0 copy-done.1
  80.5 5.3 %solve.1 = f32[128,128]{1,0:T(8,128)} custom-call(f32[8,272,128]{2,1,0:T(8,128)S(1)} %all_to_all.11.tiles_ref, bf16[16,128,128]{2,1,0:T(8,128)(2,1)S(1)} %bitcast.6, f32[128,128]{1,0:T(8,128)S(1)} %copy-done.1), custom_call_target="tpu_custom_call" | custom-call | tf_op jit(solution)/shard_map/solve/pallas_call | solution.py:221
  (4 shorter events, 0.1 us)
Async XLA Ops:
  2.5 39.2 %copy-start.2 = (s32[1,16]{1,0:T(1,128)S(1)}, s32[1,16]{1,0:T(1,128)}, u32[]{:S(2)}) copy-start(s32[1,16]{1,0:T(1,128)} %param.5) | copy-start | bytes 196
  39.8 20.3 %collective-permute-start.3 = (f32[8,272,128]{2,1,0:T(8,128)S(1)}, f32[8,272,128]{2,1,0:T(8,128)S(1)}, u32[]{:S(2)}, u32[]{:S(2)}) collective-permute-start(f32[8,272,128]{2,1,0:T(8,128)S(1)} %all_to_all.10), channel_id=1, source_target_pairs={{0,32},{32,0},{64,96},{96,64},{128,160},{160,128},{192,224},{224,1... | collective-permute-start | bytes 3342344 | tf_op jit(solution)/shard_map/ppermute | solution.py:211
  41.7 5.5 %collective-permute-start = (s32[1,16]{1,0:T(1,128)S(1)}, s32[1,16]{1,0:T(1,128)S(1)}, u32[]{:S(2)}, u32[]{:S(2)}) collective-permute-start(s32[1,16]{1,0:T(1,128)S(1)} %copy-done.2), channel_id=1, source_target_pairs={{0,1},{1,0},{2,3},{3,2},{4,5},{5,4},{6,7},{7,6},{8,9},{9,8},{10,11... | collective-permute-start | bytes 200 | tf_op jit(solution)/shard_map/ppermute | solution.py:207
  47.2 7.0 %collective-permute-start.1 = (s32[2,16]{1,0:T(2,128)S(1)}, s32[2,16]{1,0:T(2,128)S(1)}, u32[]{:S(2)}, u32[]{:S(2)}) collective-permute-start(s32[2,16]{1,0:T(2,128)S(1)} %pad_add_fusion.2), channel_id=1, source_target_pairs={{0,2},{1,3},{2,0},{3,1},{4,6},{5,7},{6,4},{7,5},{8,10},{9,11},{10,... | collective-permute-start | bytes 392 | tf_op jit(solution)/shard_map/ppermute | solution.py:207
  54.1 5.8 %collective-permute-start.2 = (s32[4,16]{1,0:T(4,128)S(1)}, s32[4,16]{1,0:T(4,128)S(1)}, u32[]{:S(2)}, u32[]{:S(2)}) collective-permute-start(s32[4,16]{1,0:T(4,128)S(1)} %pad_add_fusion.1), channel_id=1, source_target_pairs={{0,4},{1,5},{2,6},{3,7},{4,0},{5,1},{6,2},{7,3},{8,12},{9,13},{10,... | collective-permute-start | bytes 776 | tf_op jit(solution)/shard_map/ppermute | solution.py:207
  61.0 19.5 %copy-start = (bf16[1,16,128,128]{3,2,1,0:T(8,128)(2,1)S(1)}, bf16[1,16,128,128]{3,2,1,0:T(8,128)(2,1)}, u32[]{:S(2)}) copy-start(bf16[1,16,128,128]{3,2,1,0:T(8,128)(2,1)} %param.6) | copy-start | bytes 1572868
  61.1 19.5 %copy-start.1 = (f32[128,128]{1,0:T(8,128)S(1)}, f32[128,128]{1,0:T(8,128)}, u32[]{:S(2)}) copy-start(f32[128,128]{1,0:T(8,128)} %start_ref.1) | copy-start | bytes 196612

commit v4 on v3

--- a/solution.py
+++ b/solution.py
@@ -10,9 +10,10 @@
 RIDGE_WEIGHT = 0.1
 EPSILON = 1e-06
 TILE = 128
-NEAR = 8
+ROWS = 8
+PLANE = 8
+NEAR = 2 * PLANE
 SLICE = TILE // NEAR
-ROWS = 8
 PIECES = 2
 
 
@@ -28,25 +29,28 @@
 
 
 def prep_kernel(place_ref, shard_ref, out_ref, held_ref, stage_ref, gram_ref, load_sems, slice_sem, out_sem):
-    start = pl.multiple_of(place_ref[0] * SLICE, SLICE)
     rows = shard_ref.shape[0]
     tiles = rows // TILE
     part = rows // PIECES
     body, tail = pl.ds(0, tiles * SLICE), pl.ds(tiles * SLICE, SLICE)
+    starts = [pl.multiple_of((b * PLANE + place_ref[0]) * SLICE, SLICE) for b in range(2)]
 
     def load(p):
         at = pl.ds(p * part, part)
         return pltpu.make_async_copy(shard_ref.at[at], held_ref.at[at], load_sems.at[p])
 
-    for t in range(tiles):
-        pltpu.make_async_copy(
-            shard_ref.at[pl.ds(t * TILE + start, SLICE)], stage_ref.at[pl.ds(t * SLICE, SLICE)], slice_sem
-        ).start()
+    for b in range(2):
+        for t in range(tiles):
+            pltpu.make_async_copy(
+                shard_ref.at[pl.ds(t * TILE + starts[b], SLICE)],
+                stage_ref.at[b, pl.ds(t * SLICE, SLICE)],
+                slice_sem,
+            ).start()
     for p in range(PIECES):
         load(p).start()
-    pltpu.make_async_copy(shard_ref.at[body], stage_ref.at[body], slice_sem).wait()
-    for d in range(out_ref.shape[0]):
-        pltpu.make_async_copy(stage_ref.at[body], out_ref.at[d, body], out_sem).start()
+    pltpu.make_async_copy(stage_ref.at[:, body], stage_ref.at[:, body], slice_sem).wait()
+    for d in range(ROWS):
+        pltpu.make_async_copy(stage_ref.at[d % 2, body], out_ref.at[d, body], out_sem).start()
     gram = None
     for p in range(PIECES):
         load(p).wait()
@@ -56,28 +60,29 @@
         )
         gram = more if gram is None else gram + more
     gram_ref[...] = quadrants(gram)
-    stage_ref[tail, :] = gram_ref[pl.ds(start, SLICE), :]
-    for d in range(out_ref.shape[0]):
-        pltpu.make_async_copy(stage_ref.at[tail], out_ref.at[d, tail], out_sem).start()
+    for b in range(2):
+        stage_ref[b, tail, :] = gram_ref[pl.ds(starts[b], SLICE), :]
+    for d in range(ROWS):
+        pltpu.make_async_copy(stage_ref.at[d % 2, tail], out_ref.at[d, tail], out_sem).start()
     pltpu.make_async_copy(out_ref, out_ref, out_sem).wait()
 
 
 def pick_kernel(place_ref, at_ref, same_ref, mine_ref, other_ref, out_ref):
     near, slots = at_ref.shape
     place = place_ref[0]
-    step = (mine_ref.shape[0] // ROWS) - SLICE
+    block = mine_ref.shape[0] // ROWS
     gram = None
     for y in range(ROWS):
-        at = pl.ds(y * (step + SLICE) + step, SLICE)
+        at = pl.ds((y + 1) * block - SLICE, SLICE)
         more = mine_ref[at, :] + other_ref[at, :]
         gram = more if gram is None else gram + more
 
-    def one(d, _):
-        to = place ^ d
+    def one(m, _):
+        to = place ^ (((m & 1) << 3) | ((m >> 1) & 3) | ((m >> 3) << 2))
         for k in range(slots):
-            at = pl.ds(pl.multiple_of(at_ref[d, k], SLICE), SLICE)
+            at = pl.ds(pl.multiple_of(at_ref[m, k], SLICE), SLICE)
             a, b = mine_ref[at, :], other_ref[at, :]
-            out_ref[to, k * SLICE:(k + 1) * SLICE, :] = jnp.where(same_ref[d, k] != 0, a, b)
+            out_ref[to, k * SLICE:(k + 1) * SLICE, :] = jnp.where(same_ref[m, k] != 0, a, b)
         out_ref[to, slots * SLICE:, :] = gram
         return 0
 
@@ -91,11 +96,13 @@
     chunk = 2 * TILE
 
     for k in range(slots + 1):
-        for p in range(near):
-            high, low = halves(tiles_ref[p, k * SLICE:(k + 1) * SLICE, :])
+        rows = slice(k * SLICE, (k + 1) * SLICE)
+        for p in range(0, near, 2):
+            pair = jnp.concatenate([tiles_ref[p, rows, :], tiles_ref[p + 1, rows, :]], axis=0)
+            high, low = halves(pair)
             at = k * TILE + p * SLICE
-            y_ref[at:at + SLICE, :TILE] = high
-            y_ref[at:at + SLICE, TILE:] = low
+            y_ref[at:at + 2 * SLICE, :TILE] = high
+            y_ref[at:at + 2 * SLICE, TILE:] = low
 
     def wide(n):
         pair = jnp.concatenate([weights_ref[2 * n], weights_ref[2 * n + 1]], axis=1)
@@ -176,35 +183,45 @@
     slots = tile_lists.shape[1]
     shards = lax.axis_size("item")
     users = lax.axis_size("user")
-    rows_y = shards // 2
-    assert rows_y == ROWS
-    column = [[2 * y + c for y in range(rows_y)] for c in range(2)]
-    around = [[g * NEAR + j for j in range(NEAR)] for g in range(users // NEAR)]
+    assert shards == 2 * ROWS and users % PLANE == 0
+    column = [[2 * y + c for y in range(ROWS)] for c in range(2)]
+    around = [
+        [(2 * (y + b) + c) * users + z * PLANE + r for b in range(2) for r in range(PLANE)]
+        for y in range(0, ROWS, 2) for c in range(2) for z in range(users // PLANE)
+    ]
     swap = [(i, i ^ 1) for i in range(shards)]
-    place = (lax.axis_index("user") % NEAR).astype(jnp.int32).reshape(1)
-    core = (lax.axis_index("item") % 2).astype(jnp.int32).reshape(1)
+    item, user = lax.axis_index("item"), lax.axis_index("user")
+    core = item & 1
+    beside = (user & (PLANE - 1)).reshape(1)
+    place = (((item >> 1) & 1) * PLANE + (user & (PLANE - 1))).reshape(1)
     held = item_factors.shape[0] // TILE
 
+    pair_lists = jnp.concatenate(
+        [tile_lists, lax.ppermute(tile_lists, "item", [(i, i ^ 2) for i in range(shards)])], axis=0
+    )
     send_a = pl.pallas_call(
         prep_kernel,
-        out_shape=jax.ShapeDtypeStruct((rows_y, (held + 1) * SLICE, rank), jnp.float32),
+        out_shape=jax.ShapeDtypeStruct((ROWS, (held + 1) * SLICE, rank), jnp.float32),
         in_specs=[SMEM, pl.BlockSpec(memory_space=pltpu.MemorySpace.HBM)],
         out_specs=pl.BlockSpec(memory_space=pltpu.MemorySpace.HBM),
         scratch_shapes=[
             pltpu.VMEM(item_factors.shape, jnp.float32),
-            pltpu.VMEM(((held + 1) * SLICE, rank), jnp.float32),
+            pltpu.VMEM((2, (held + 1) * SLICE, rank), jnp.float32),
             pltpu.VMEM((rank, rank), jnp.float32),
             pltpu.SemaphoreType.DMA((PIECES,)),
             pltpu.SemaphoreType.DMA,
             pltpu.SemaphoreType.DMA,
         ],
         name="prep",
-    )(place, item_factors)
+    )(beside, item_factors)
     mine = lax.all_to_all(send_a, "item", 0, 0, tiled=True, axis_index_groups=column)
-    near_lists = tile_lists
-    for bit in (1, 2, 4):
-        step = [(u, u ^ bit) for u in range(users)]
-        near_lists = jnp.concatenate([near_lists, lax.ppermute(near_lists, "user", step)], axis=0)
+    quad = [pair_lists] + [
+        lax.ppermute(pair_lists, "user", [(u, u ^ x) for u in range(users)]) for x in range(1, 4)
+    ]
+    quad = jnp.concatenate(quad, axis=0)
+    near_lists = jnp.concatenate(
+        [quad, lax.ppermute(quad, "user", [(u, u ^ 4) for u in range(users)])], axis=0
+    )
     shard = near_lists // held
     at = ((shard // 2) * (held + 1) + near_lists % held) * SLICE
     same = (shard % 2 == core).astype(jnp.int32)
@@ -217,7 +234,7 @@
         compiler_params=grant(12),
         name="pick",
     )(place, at, same, mine.reshape(-1, rank), other.reshape(-1, rank))
-    tiles = lax.all_to_all(send_b, "user", 0, 0, tiled=True, axis_index_groups=around)
+    tiles = lax.all_to_all(send_b, ("item", "user"), 0, 0, tiled=True, axis_index_groups=around)
     return pl.pallas_call(
         solve_kernel,
         out_shape=jax.ShapeDtypeStruct((TILE, rank), jnp.float32),

time: 86.2 us -> 76.7 us (0.89)
  blocking collectives: 56.7 us -> 20.8 us
  waiting for transfers between devices: 5.63 us -> 18.8 us
  starting transfers between devices: 14.5 us -> 27 us
    all_to_all x2 -> x1, blocking collectives: 56.7 us -> 20.8 us  [chain(): lax.all_to_all(send_b, ('item', 'user'), 0, 0, tiled=True, axis_index_gro...]
    all_to_all x0 -> x1, waiting for transfers between devices: none -> 14.3 us  [chain(): lax.all_to_all(send_a, 'item', 0, 0, tiled=True, axis_index_groups=column)]
    all_to_all x0 -> x1, starting transfers between devices: none -> 7.11 us  [chain(): lax.all_to_all(send_a, 'item', 0, 0, tiled=True, axis_index_groups=column)]
    ppermute x3 -> x5, starting transfers between devices: 12.6 us -> 18 us  [the longest x3 9.82 us: chain(): lax.ppermute(pair_lists, 'user', [(u, u ^ x) for u in range(users)])]
    ppermute x3 -> x5, waiting for transfers between devices: 5.63 us -> 4.57 us  [the longest x3 3.01 us: chain(): lax.ppermute(pair_lists, 'user', [(u, u ^ x) for u in range(users)])]
  transfers between devices with their start and end apart: 4 -> 7, of which waited for: 3 -> 4; matrix products, arithmetic and copies ran while one was open for 0% -> 0% of each run, Pallas kernels for 0% -> 0%
where the time goes in v4:
time: 76.7 us; the launch traced here: 76.3 us
  starting transfers between devices  27 us (35%)
  blocking collectives  20.8 us (27%)
  waiting for transfers between devices  18.8 us (25%)
  Pallas kernels  9.34 us (12%)
    all_to_all x1, blocking collectives, chain(): lax.all_to_all(send_b, ('item', 'user'), 0, 0, tiled=True, axis_index_gro...  20.8 us
    all_to_all x1, waiting for transfers between devices, chain(): lax.all_to_all(send_a, 'item', 0, 0, tiled=True, axis_index_groups=column)  14.3 us
    ppermute x3, starting transfers between devices, chain(): lax.ppermute(pair_lists, 'user', [(u, u ^ x) for u in range(users)])  9.82 us
    all_to_all x1, starting transfers between devices, chain(): lax.all_to_all(send_a, 'item', 0, 0, tiled=True, axis_index_groups=column)  7.11 us
    pallas_call x1, Pallas kernels, chain(): pl.pallas_call(solve_kernel, out_shape=jax.ShapeDtypeStruct((TILE, rank),...  5.32 us
    ppermute x1, starting transfers between devices, chain(): lax.ppermute(quad, 'user', [(u, u ^ 4) for u in range(users)])  4.28 us
    ppermute x1, starting transfers between devices, chain(): lax.ppermute(tile_lists, 'item', [(i, i ^ 2) for i in range(shards)])  3.92 us
    ppermute x3, waiting for transfers between devices, chain(): lax.ppermute(pair_lists, 'user', [(u, u ^ x) for u in range(users)])  3.01 us
  transfers between devices with their start and end apart: 7, of which 4 were waited for; matrix products, arithmetic and copies ran while one was open for 0% of the time, Pallas kernels for 0%

profile of v4, /device:TPU:128, one launch (start us, length us, event | category | flops | bytes accessed | tf_op | source)
XLA Modules:
  0.0 76.3 jit_solution(15317936279019311962)
XLA Ops:
  0.0 0.0 copy-start.2
  0.0 2.5 %prep.1 = f32[8,136,128]{2,1,0:T(8,128)} custom-call(s32[1]{0:T(128)} %bitcast.1.place_ref, f32[2048,128]{1,0:T(8,128)} %shard_ref.1), custom_call_target="tpu_custom_call" | custom-call | tf_op jit(solution)/shard_map/prep/pallas_call | solution.py:202
  2.6 7.1 %all-to-all-start = ((f32[8,136,128]{2,1,0:T(8,128)}), f32[8,136,128]{2,1,0:T(8,128)S(1)}, u32[]{:S(2)}, u32[]{:S(2)}) async-start(f32[8,136,128]{2,1,0:T(8,128)} %prep.1), calls=%async_computation | async-start | bytes 1114112 | tf_op jit(solution)/shard_map/all_to_all | solution.py:217
  9.7 0.0 copy-done.2
  9.7 3.9 %collective-permute-start = (s32[1,16]{1,0:T(1,128)S(1)}, s32[1,16]{1,0:T(1,128)S(1)}, u32[]{:S(2)}, u32[]{:S(2)}) collective-permute-start(s32[1,16]{1,0:T(1,128)S(1)} %copy-done.2), channel_id=1, source_target_pairs={{0,64},{32,96},{64,0},{96,32},{128,192},{160,224},{192,128},{224,1... | collective-permute-start | bytes 200 | tf_op jit(solution)/shard_map/ppermute | solution.py:200
  13.6 14.3 %all-to-all-done = f32[8,136,128]{2,1,0:T(8,128)S(1)} async-done(((f32[8,136,128]{2,1,0:T(8,128)}), f32[8,136,128]{2,1,0:T(8,128)S(1)}, u32[]{:S(2)}, u32[]{:S(2)}) %all-to-all-start) | async-done | bytes 557088 | tf_op jit(solution)/shard_map/all_to_all | solution.py:217
  27.9 1.9 %collective-permute-start.5 = (f32[8,136,128]{2,1,0:T(8,128)S(1)}, f32[8,136,128]{2,1,0:T(8,128)S(1)}, u32[]{:S(2)}, u32[]{:S(2)}) collective-permute-start(f32[8,136,128]{2,1,0:T(8,128)S(1)} %all-to-all-done), channel_id=1, source_target_pairs={{0,32},{32,0},{64,96},{96,64},{128,160},{160,128},{192,224},{224,1... | collective-permute-start | bytes 1671176 | tf_op jit(solution)/shard_map/ppermute | solution.py:228
  29.8 0.0 collective-permute-done
  29.8 4.7 %collective-permute-start.3 = (s32[2,16]{1,0:T(2,128)S(1)}, s32[2,16]{1,0:T(2,128)S(1)}, u32[]{:S(2)}, u32[]{:S(2)}) collective-permute-start(s32[2,16]{1,0:T(2,128)S(1)} %pad_add_fusion), channel_id=1, source_target_pairs={{0,3},{1,2},{2,1},{3,0},{4,7},{5,6},{6,5},{7,4},{8,11},{9,10},{10,... | collective-permute-start | bytes 392 | tf_op jit(solution)/shard_map/ppermute | solution.py:219
  34.5 2.7 %collective-permute-start.2 = (s32[2,16]{1,0:T(2,128)S(1)}, s32[2,16]{1,0:T(2,128)S(1)}, u32[]{:S(2)}, u32[]{:S(2)}) collective-permute-start(s32[2,16]{1,0:T(2,128)S(1)} %pad_add_fusion), channel_id=1, source_target_pairs={{0,2},{1,3},{2,0},{3,1},{4,6},{5,7},{6,4},{7,5},{8,10},{9,11},{10,... | collective-permute-start | bytes 392 | tf_op jit(solution)/shard_map/ppermute | solution.py:219
  37.2 2.4 %collective-permute-start.1 = (s32[2,16]{1,0:T(2,128)S(1)}, s32[2,16]{1,0:T(2,128)S(1)}, u32[]{:S(2)}, u32[]{:S(2)}) collective-permute-start(s32[2,16]{1,0:T(2,128)S(1)} %pad_add_fusion), channel_id=1, source_target_pairs={{0,1},{1,0},{2,3},{3,2},{4,5},{5,4},{6,7},{7,6},{8,9},{9,8},{10,11... | collective-permute-start | bytes 392 | tf_op jit(solution)/shard_map/ppermute | solution.py:219
  39.7 0.0 collective-permute-done.3
  39.7 1.8 %collective-permute-done.2 = s32[2,16]{1,0:T(2,128)S(1)} collective-permute-done((s32[2,16]{1,0:T(2,128)S(1)}, s32[2,16]{1,0:T(2,128)S(1)}, u32[]{:S(2)}, u32[]{:S(2)}) %collective-permute-start.2) | collective-permute-done | bytes 160 | tf_op jit(solution)/shard_map/ppermute | solution.py:219
  41.5 1.2 %collective-permute-done.1 = s32[2,16]{1,0:T(2,128)S(1)} collective-permute-done((s32[2,16]{1,0:T(2,128)S(1)}, s32[2,16]{1,0:T(2,128)S(1)}, u32[]{:S(2)}, u32[]{:S(2)}) %collective-permute-start.1) | collective-permute-done | bytes 160 | tf_op jit(solution)/shard_map/ppermute | solution.py:219
  42.7 4.3 %collective-permute-start.4 = (s32[8,16]{1,0:T(8,128)S(1)}, s32[8,16]{1,0:T(8,128)S(1)}, u32[]{:S(2)}, u32[]{:S(2)}) collective-permute-start(s32[8,16]{1,0:T(8,128)S(1)} %concatenate.12), channel_id=1, source_target_pairs={{0,4},{1,5},{2,6},{3,7},{4,0},{5,1},{6,2},{7,3},{8,12},{9,13},{10,... | collective-permute-start | bytes 1544 | tf_op jit(solution)/shard_map/ppermute | solution.py:223
  47.0 1.6 %collective-permute-done.4 = s32[8,16]{1,0:T(8,128)S(1)} collective-permute-done((s32[8,16]{1,0:T(8,128)S(1)}, s32[8,16]{1,0:T(8,128)S(1)}, u32[]{:S(2)}, u32[]{:S(2)}) %collective-permute-start.4) | collective-permute-done | bytes 544 | tf_op jit(solution)/shard_map/ppermute | solution.py:223
  48.6 0.0 collective-permute-done.5
  48.6 1.5 %pick.1 = f32[16,136,128]{2,1,0:T(8,128)S(1)} custom-call(s32[1]{0:T(128)} %bitcast.place_ref, s32[16,16]{1,0:T(8,128)S(1)} %fusion.2.at_ref, s32[16,16]{1,0:T(8,128)S(1)} %fusion.6.same_ref, f32[1088,128]{1,0:T(8,128)S(1)} %bitcast.5, f32[1088,128]{1,0:T(8,128)S(1)} %bitcast.6), custom_call_target="tpu_custom_call" | custom-call | tf_op jit(solution)/shard_map/pick/pallas_call | solution.py:229
  50.1 0.0 copy-start
  50.1 0.0 copy-start.1
  50.1 20.8 %all_to_all.10.tiles_ref = f32[16,136,128]{2,1,0:T(8,128)S(1)} all-to-all(f32[16,136,128]{2,1,0:T(8,128)S(1)} %pick.1), channel_id=1, replica_groups={{0,1,2,3,4,5,6,7,64,65,66,67,68,69,70,71},{8,9,10,11,12,13,14,15,72,73,..., dimensions={0} | all-to-all | bytes 2228224 | tf_op jit(solution)/shard_map/all_to_all | solution.py:237
  70.9 0.0 copy-done
  70.9 0.0 copy-done.1
  70.9 5.3 %solve.1 = f32[128,128]{1,0:T(8,128)} custom-call(f32[16,136,128]{2,1,0:T(8,128)S(1)} %all_to_all.10.tiles_ref, bf16[16,128,128]{2,1,0:T(8,128)(2,1)S(1)} %bitcast.7, f32[128,128]{1,0:T(8,128)S(1)} %copy-done.1), custom_call_target="tpu_custom_call" | custom-call | tf_op jit(solution)/shard_map/solve/pallas_call | solution.py:238
  (5 shorter events, 0.1 us)
Async XLA Ops:
  0.0 9.7 %copy-start.2 = (s32[1,16]{1,0:T(1,128)S(1)}, s32[1,16]{1,0:T(1,128)}, u32[]{:S(2)}) copy-start(s32[1,16]{1,0:T(1,128)} %param.5) | copy-start | bytes 196
  2.6 25.3 %all-to-all-start = ((f32[8,136,128]{2,1,0:T(8,128)}), f32[8,136,128]{2,1,0:T(8,128)S(1)}, u32[]{:S(2)}, u32[]{:S(2)}) async-start(f32[8,136,128]{2,1,0:T(8,128)} %prep.1), calls=%async_computation | async-start | bytes 1114112 | tf_op jit(solution)/shard_map/all_to_all | solution.py:217
  9.7 20.1 %collective-permute-start = (s32[1,16]{1,0:T(1,128)S(1)}, s32[1,16]{1,0:T(1,128)S(1)}, u32[]{:S(2)}, u32[]{:S(2)}) collective-permute-start(s32[1,16]{1,0:T(1,128)S(1)} %copy-done.2), channel_id=1, source_target_pairs={{0,64},{32,96},{64,0},{96,32},{128,192},{160,224},{192,128},{224,1... | collective-permute-start | bytes 200 | tf_op jit(solution)/shard_map/ppermute | solution.py:200
  27.9 20.8 %collective-permute-start.5 = (f32[8,136,128]{2,1,0:T(8,128)S(1)}, f32[8,136,128]{2,1,0:T(8,128)S(1)}, u32[]{:S(2)}, u32[]{:S(2)}) collective-permute-start(f32[8,136,128]{2,1,0:T(8,128)S(1)} %all-to-all-done), channel_id=1, source_target_pairs={{0,32},{32,0},{64,96},{96,64},{128,160},{160,128},{192,224},{224,1... | collective-permute-start | bytes 1671176 | tf_op jit(solution)/shard_map/ppermute | solution.py:228
  29.8 9.8 %collective-permute-start.3 = (s32[2,16]{1,0:T(2,128)S(1)}, s32[2,16]{1,0:T(2,128)S(1)}, u32[]{:S(2)}, u32[]{:S(2)}) collective-permute-start(s32[2,16]{1,0:T(2,128)S(1)} %pad_add_fusion), channel_id=1, source_target_pairs={{0,3},{1,2},{2,1},{3,0},{4,7},{5,6},{6,5},{7,4},{8,11},{9,10},{10,... | collective-permute-start | bytes 392 | tf_op jit(solution)/shard_map/ppermute | solution.py:219
  34.5 7.0 %collective-permute-start.2 = (s32[2,16]{1,0:T(2,128)S(1)}, s32[2,16]{1,0:T(2,128)S(1)}, u32[]{:S(2)}, u32[]{:S(2)}) collective-permute-start(s32[2,16]{1,0:T(2,128)S(1)} %pad_add_fusion), channel_id=1, source_target_pairs={{0,2},{1,3},{2,0},{3,1},{4,6},{5,7},{6,4},{7,5},{8,10},{9,11},{10,... | collective-permute-start | bytes 392 | tf_op jit(solution)/shard_map/ppermute | solution.py:219
  37.2 5.5 %collective-permute-start.1 = (s32[2,16]{1,0:T(2,128)S(1)}, s32[2,16]{1,0:T(2,128)S(1)}, u32[]{:S(2)}, u32[]{:S(2)}) collective-permute-start(s32[2,16]{1,0:T(2,128)S(1)} %pad_add_fusion), channel_id=1, source_target_pairs={{0,1},{1,0},{2,3},{3,2},{4,5},{5,4},{6,7},{7,6},{8,9},{9,8},{10,11... | collective-permute-start | bytes 392 | tf_op jit(solution)/shard_map/ppermute | solution.py:219
  42.7 5.9 %collective-permute-start.4 = (s32[8,16]{1,0:T(8,128)S(1)}, s32[8,16]{1,0:T(8,128)S(1)}, u32[]{:S(2)}, u32[]{:S(2)}) collective-permute-start(s32[8,16]{1,0:T(8,128)S(1)} %concatenate.12), channel_id=1, source_target_pairs={{0,4},{1,5},{2,6},{3,7},{4,0},{5,1},{6,2},{7,3},{8,12},{9,13},{10,... | collective-permute-start | bytes 1544 | tf_op jit(solution)/shard_map/ppermute | solution.py:223
  50.1 20.8 %copy-start = (bf16[1,16,128,128]{3,2,1,0:T(8,128)(2,1)S(1)}, bf16[1,16,128,128]{3,2,1,0:T(8,128)(2,1)}, u32[]{:S(2)}) copy-start(bf16[1,16,128,128]{3,2,1,0:T(8,128)(2,1)} %param.6) | copy-start | bytes 1572868
  50.1 20.8 %copy-start.1 = (f32[128,128]{1,0:T(8,128)S(1)}, f32[128,128]{1,0:T(8,128)}, u32[]{:S(2)}) copy-start(f32[128,128]{1,0:T(8,128)} %start_ref.1) | copy-start | bytes 196612

commit v5 on v4

--- a/solution.py
+++ b/solution.py
@@ -14,7 +14,6 @@
 PLANE = 8
 NEAR = 2 * PLANE
 SLICE = TILE // NEAR
-PIECES = 2
 
 
 def halves(x):
@@ -28,37 +27,19 @@
     return (x[:rows, :cols] + x[:rows, cols:]) + (x[rows:, :cols] + x[rows:, cols:])
 
 
-def prep_kernel(place_ref, shard_ref, out_ref, held_ref, stage_ref, gram_ref, load_sems, slice_sem, out_sem):
+def prep_kernel(place_ref, shard_ref, out_ref, stage_ref, gram_ref, out_sem):
     rows = shard_ref.shape[0]
     tiles = rows // TILE
-    part = rows // PIECES
     body, tail = pl.ds(0, tiles * SLICE), pl.ds(tiles * SLICE, SLICE)
     starts = [pl.multiple_of((b * PLANE + place_ref[0]) * SLICE, SLICE) for b in range(2)]
 
-    def load(p):
-        at = pl.ds(p * part, part)
-        return pltpu.make_async_copy(shard_ref.at[at], held_ref.at[at], load_sems.at[p])
-
     for b in range(2):
         for t in range(tiles):
-            pltpu.make_async_copy(
-                shard_ref.at[pl.ds(t * TILE + starts[b], SLICE)],
-                stage_ref.at[b, pl.ds(t * SLICE, SLICE)],
-                slice_sem,
-            ).start()
-    for p in range(PIECES):
-        load(p).start()
-    pltpu.make_async_copy(stage_ref.at[:, body], stage_ref.at[:, body], slice_sem).wait()
+            stage_ref[b, t * SLICE:(t + 1) * SLICE, :] = shard_ref[pl.ds(t * TILE + starts[b], SLICE), :]
     for d in range(ROWS):
         pltpu.make_async_copy(stage_ref.at[d % 2, body], out_ref.at[d, body], out_sem).start()
-    gram = None
-    for p in range(PIECES):
-        load(p).wait()
-        both = jnp.concatenate(halves(held_ref[p * part:(p + 1) * part, :]), axis=1)
-        more = lax.dot_general(
-            both, both, (((0,), (0,)), ((), ())), preferred_element_type=jnp.float32
-        )
-        gram = more if gram is None else gram + more
+    both = jnp.concatenate(halves(shard_ref[...]), axis=1)
+    gram = lax.dot_general(both, both, (((0,), (0,)), ((), ())), preferred_element_type=jnp.float32)
     gram_ref[...] = quadrants(gram)
     for b in range(2):
         stage_ref[b, tail, :] = gram_ref[pl.ds(starts[b], SLICE), :]
@@ -67,22 +48,23 @@
     pltpu.make_async_copy(out_ref, out_ref, out_sem).wait()
 
 
-def pick_kernel(place_ref, at_ref, same_ref, mine_ref, other_ref, out_ref):
+def pick_kernel(place_ref, at_ref, mine_ref, other_ref, out_ref, both_ref):
     near, slots = at_ref.shape
     place = place_ref[0]
-    block = mine_ref.shape[0] // ROWS
+    rows = mine_ref.shape[0]
+    block = rows // ROWS
+    both_ref[:rows, :] = mine_ref[...]
+    both_ref[rows:, :] = other_ref[...]
     gram = None
-    for y in range(ROWS):
-        at = pl.ds((y + 1) * block - SLICE, SLICE)
-        more = mine_ref[at, :] + other_ref[at, :]
+    for y in range(2 * ROWS):
+        more = both_ref[(y + 1) * block - SLICE:(y + 1) * block, :]
         gram = more if gram is None else gram + more
 
     def one(m, _):
         to = place ^ (((m & 1) << 3) | ((m >> 1) & 3) | ((m >> 3) << 2))
         for k in range(slots):
             at = pl.ds(pl.multiple_of(at_ref[m, k], SLICE), SLICE)
-            a, b = mine_ref[at, :], other_ref[at, :]
-            out_ref[to, k * SLICE:(k + 1) * SLICE, :] = jnp.where(same_ref[m, k] != 0, a, b)
+            out_ref[to, k * SLICE:(k + 1) * SLICE, :] = both_ref[at, :]
         out_ref[to, slots * SLICE:, :] = gram
         return 0
 
@@ -202,16 +184,14 @@
     send_a = pl.pallas_call(
         prep_kernel,
         out_shape=jax.ShapeDtypeStruct((ROWS, (held + 1) * SLICE, rank), jnp.float32),
-        in_specs=[SMEM, pl.BlockSpec(memory_space=pltpu.MemorySpace.HBM)],
+        in_specs=[SMEM, VMEM],
         out_specs=pl.BlockSpec(memory_space=pltpu.MemorySpace.HBM),
         scratch_shapes=[
-            pltpu.VMEM(item_factors.shape, jnp.float32),
             pltpu.VMEM((2, (held + 1) * SLICE, rank), jnp.float32),
             pltpu.VMEM((rank, rank), jnp.float32),
-            pltpu.SemaphoreType.DMA((PIECES,)),
-            pltpu.SemaphoreType.DMA,
             pltpu.SemaphoreType.DMA,
         ],
+        compiler_params=grant(16),
         name="prep",
     )(beside, item_factors)
     mine = lax.all_to_all(send_a, "item", 0, 0, tiled=True, axis_index_groups=column)
@@ -223,17 +203,18 @@
         [quad, lax.ppermute(quad, "user", [(u, u ^ 4) for u in range(users)])], axis=0
     )
     shard = near_lists // held
-    at = ((shard // 2) * (held + 1) + near_lists % held) * SLICE
-    same = (shard % 2 == core).astype(jnp.int32)
+    half = jnp.where(shard % 2 == core, 0, ROWS)
+    at = ((half + shard // 2) * (held + 1) + near_lists % held) * SLICE
     other = lax.ppermute(mine, "item", swap)
     send_b = pl.pallas_call(
         pick_kernel,
         out_shape=jax.ShapeDtypeStruct((NEAR, (slots + 1) * SLICE, rank), jnp.float32),
-        in_specs=[SMEM, SMEM, SMEM, VMEM, VMEM],
+        in_specs=[SMEM, SMEM, VMEM, VMEM],
         out_specs=VMEM,
+        scratch_shapes=[pltpu.VMEM((2 * ROWS * (held + 1) * SLICE, rank), jnp.float32)],
         compiler_params=grant(12),
         name="pick",
-    )(place, at, same, mine.reshape(-1, rank), other.reshape(-1, rank))
+    )(place, at, mine.reshape(-1, rank), other.reshape(-1, rank))
     tiles = lax.all_to_all(send_b, ("item", "user"), 0, 0, tiled=True, axis_index_groups=around)
     return pl.pallas_call(
         solve_kernel,

time: 76.7 us -> 80.2 us (1.046)
  blocking collectives: 20.8 us -> 44.7 us
  waiting for transfers between devices: 18.8 us -> 7.55 us
  starting transfers between devices: 27 us -> 18.5 us
  Pallas kernels: 9.34 us -> 7.61 us
  local copies, waits for them, and re-layouts: 0.06 us -> 1.28 us
    all_to_all x0 -> x1, blocking collectives: none -> 25.1 us  [chain(): lax.all_to_all(send_a, 'item', 0, 0, tiled=True, axis_index_groups=column)]
    all_to_all x1 -> x0, waiting for transfers between devices: 14.3 us -> none  [chain(): lax.all_to_all(send_a, 'item', 0, 0, tiled=True, axis_index_groups=column)]
    all_to_all x1 -> x0, starting transfers between devices: 7.11 us -> none  [chain(): lax.all_to_all(send_a, 'item', 0, 0, tiled=True, axis_index_groups=column)]
    ppermute x1, waiting for transfers between devices: 0.01 us -> 2.98 us  [chain(): lax.ppermute(tile_lists, 'item', [(i, i ^ 2) for i in range(shards)])]
    ppermute x1, starting transfers between devices: 3.92 us -> 2.47 us  [chain(): lax.ppermute(tile_lists, 'item', [(i, i ^ 2) for i in range(shards)])]
    pallas_call x1, Pallas kernels: 2.55 us -> 1.23 us  [chain(): pl.pallas_call(prep_kernel, out_shape=jax.ShapeDtypeStruct((ROWS, (held +...]
    unnamed x6 -> x8, local copies, waits for them, and re-layouts: 0.02 us -> 1.24 us
    all_to_all x1, blocking collectives: 20.8 us -> 19.7 us  [chain(): lax.all_to_all(send_b, ('item', 'user'), 0, 0, tiled=True, axis_index_gro...]
  transfers between devices with their start and end apart: 7 -> 6, of which waited for: 4 -> 4; matrix products, arithmetic and copies ran while one was open for 0% -> 0% of each run, Pallas kernels for 0% -> 0%
where the time goes in v5:
time: 80.2 us; the launch traced here: 79.8 us
  blocking collectives  44.7 us (56%)
  starting transfers between devices  18.5 us (23%)
  Pallas kernels  7.61 us (9%)
  waiting for transfers between devices  7.55 us (9%)
  local copies, waits for them, and re-layouts  1.28 us (2%)
    all_to_all x1, blocking collectives, chain(): lax.all_to_all(send_a, 'item', 0, 0, tiled=True, axis_index_groups=column)  25.1 us
    all_to_all x1, blocking collectives, chain(): lax.all_to_all(send_b, ('item', 'user'), 0, 0, tiled=True, axis_index_gro...  19.7 us
    ppermute x3, starting transfers between devices, chain(): lax.ppermute(pair_lists, 'user', [(u, u ^ x) for u in range(users)])  9.81 us
    pallas_call x1, Pallas kernels, chain(): pl.pallas_call(solve_kernel, out_shape=jax.ShapeDtypeStruct((TILE, rank),...  5.32 us
    ppermute x1, starting transfers between devices, chain(): lax.ppermute(quad, 'user', [(u, u ^ 4) for u in range(users)])  4.27 us
    ppermute x3, waiting for transfers between devices, chain(): lax.ppermute(pair_lists, 'user', [(u, u ^ x) for u in range(users)])  3.01 us
    ppermute x1, waiting for transfers between devices, chain(): lax.ppermute(tile_lists, 'item', [(i, i ^ 2) for i in range(shards)])  2.98 us
    ppermute x1, starting transfers between devices, chain(): lax.ppermute(tile_lists, 'item', [(i, i ^ 2) for i in range(shards)])  2.47 us
  transfers between devices with their start and end apart: 6, of which 4 were waited for; matrix products, arithmetic and copies ran while one was open for 0% of the time, Pallas kernels for 0%

profile of v5, /device:TPU:128, one launch (start us, length us, event | category | flops | bytes accessed | tf_op | source)
XLA Modules:
  0.0 79.8 jit_solution(13095151644967522367)
XLA Ops:
  0.0 0.0 copy-start
  0.0 1.2 %copy-done = f32[2048,128]{1,0:T(8,128)S(1)} copy-done((f32[2048,128]{1,0:T(8,128)S(1)}, f32[2048,128]{1,0:T(8,128)}, u32[]{:S(2)}) %copy-start) | copy-done | bytes 1048600
  1.2 0.0 copy-start.3
  1.2 1.2 %prep.1 = f32[8,136,128]{2,1,0:T(8,128)S(1)} custom-call(s32[1]{0:T(128)} %bitcast.1.place_ref, f32[2048,128]{1,0:T(8,128)S(1)} %copy-done), custom_call_target="tpu_custom_call" | custom-call | tf_op jit(solution)/shard_map/prep/pallas_call | solution.py:184
  2.5 25.1 %all_to_all.10 = f32[8,136,128]{2,1,0:T(8,128)S(1)} all-to-all(f32[8,136,128]{2,1,0:T(8,128)S(1)} %prep.1), channel_id=1, replica_groups={{0,64,128,192,256,320,384,448},{32,96,160,224,288,352,416,480},{1,65,12..., dimensions={0} | all-to-all | bytes 1114112 | tf_op jit(solution)/shard_map/all_to_all | solution.py:197
  27.6 1.9 %collective-permute-start.5 = (f32[8,136,128]{2,1,0:T(8,128)S(1)}, f32[8,136,128]{2,1,0:T(8,128)S(1)}, u32[]{:S(2)}, u32[]{:S(2)}) collective-permute-start(f32[8,136,128]{2,1,0:T(8,128)S(1)} %all_to_all.10), channel_id=1, source_target_pairs={{0,32},{32,0},{64,96},{96,64},{128,160},{160,128},{192,224},{224,1... | collective-permute-start | bytes 1671176 | tf_op jit(solution)/shard_map/ppermute | solution.py:208
  29.5 0.0 copy-done.3
  29.5 2.5 %collective-permute-start = (s32[1,16]{1,0:T(1,128)S(1)}, s32[1,16]{1,0:T(1,128)S(1)}, u32[]{:S(2)}, u32[]{:S(2)}) collective-permute-start(s32[1,16]{1,0:T(1,128)S(1)} %copy-done.3), channel_id=1, source_target_pairs={{0,64},{32,96},{64,0},{96,32},{128,192},{160,224},{192,128},{224,1... | collective-permute-start | bytes 200 | tf_op jit(solution)/shard_map/ppermute | solution.py:182
  32.0 3.0 %collective-permute-done = s32[1,16]{1,0:T(1,128)S(1)} collective-permute-done((s32[1,16]{1,0:T(1,128)S(1)}, s32[1,16]{1,0:T(1,128)S(1)}, u32[]{:S(2)}, u32[]{:S(2)}) %collective-permute-start) | collective-permute-done | bytes 96 | tf_op jit(solution)/shard_map/ppermute | solution.py:182
  35.0 4.7 %collective-permute-start.3 = (s32[2,16]{1,0:T(2,128)S(1)}, s32[2,16]{1,0:T(2,128)S(1)}, u32[]{:S(2)}, u32[]{:S(2)}) collective-permute-start(s32[2,16]{1,0:T(2,128)S(1)} %pad_add_fusion), channel_id=1, source_target_pairs={{0,3},{1,2},{2,1},{3,0},{4,7},{5,6},{6,5},{7,4},{8,11},{9,10},{10,... | collective-permute-start | bytes 392 | tf_op jit(solution)/shard_map/ppermute | solution.py:199
  39.6 2.7 %collective-permute-start.2 = (s32[2,16]{1,0:T(2,128)S(1)}, s32[2,16]{1,0:T(2,128)S(1)}, u32[]{:S(2)}, u32[]{:S(2)}) collective-permute-start(s32[2,16]{1,0:T(2,128)S(1)} %pad_add_fusion), channel_id=1, source_target_pairs={{0,2},{1,3},{2,0},{3,1},{4,6},{5,7},{6,4},{7,5},{8,10},{9,11},{10,... | collective-permute-start | bytes 392 | tf_op jit(solution)/shard_map/ppermute | solution.py:199
  42.4 2.4 %collective-permute-start.1 = (s32[2,16]{1,0:T(2,128)S(1)}, s32[2,16]{1,0:T(2,128)S(1)}, u32[]{:S(2)}, u32[]{:S(2)}) collective-permute-start(s32[2,16]{1,0:T(2,128)S(1)} %pad_add_fusion), channel_id=1, source_target_pairs={{0,1},{1,0},{2,3},{3,2},{4,5},{5,4},{6,7},{7,6},{8,9},{9,8},{10,11... | collective-permute-start | bytes 392 | tf_op jit(solution)/shard_map/ppermute | solution.py:199
  44.8 0.0 collective-permute-done.3
  44.8 1.8 %collective-permute-done.2 = s32[2,16]{1,0:T(2,128)S(1)} collective-permute-done((s32[2,16]{1,0:T(2,128)S(1)}, s32[2,16]{1,0:T(2,128)S(1)}, u32[]{:S(2)}, u32[]{:S(2)}) %collective-permute-start.2) | collective-permute-done | bytes 160 | tf_op jit(solution)/shard_map/ppermute | solution.py:199
  46.6 1.2 %collective-permute-done.1 = s32[2,16]{1,0:T(2,128)S(1)} collective-permute-done((s32[2,16]{1,0:T(2,128)S(1)}, s32[2,16]{1,0:T(2,128)S(1)}, u32[]{:S(2)}, u32[]{:S(2)}) %collective-permute-start.1) | collective-permute-done | bytes 160 | tf_op jit(solution)/shard_map/ppermute | solution.py:199
  47.8 4.3 %collective-permute-start.4 = (s32[8,16]{1,0:T(8,128)S(1)}, s32[8,16]{1,0:T(8,128)S(1)}, u32[]{:S(2)}, u32[]{:S(2)}) collective-permute-start(s32[8,16]{1,0:T(8,128)S(1)} %concatenate.12), channel_id=1, source_target_pairs={{0,4},{1,5},{2,6},{3,7},{4,0},{5,1},{6,2},{7,3},{8,12},{9,13},{10,... | collective-permute-start | bytes 1544 | tf_op jit(solution)/shard_map/ppermute | solution.py:203
  52.1 1.6 %collective-permute-done.4 = s32[8,16]{1,0:T(8,128)S(1)} collective-permute-done((s32[8,16]{1,0:T(8,128)S(1)}, s32[8,16]{1,0:T(8,128)S(1)}, u32[]{:S(2)}, u32[]{:S(2)}) %collective-permute-start.4) | collective-permute-done | bytes 544 | tf_op jit(solution)/shard_map/ppermute | solution.py:203
  53.7 0.0 collective-permute-done.5
  53.8 1.1 %pick.1 = f32[16,136,128]{2,1,0:T(8,128)S(1)} custom-call(s32[1]{0:T(128)} %bitcast.place_ref, s32[16,16]{1,0:T(8,128)S(1)} %fusion.4.at_ref, f32[1088,128]{1,0:T(8,128)S(1)} %bitcast.5, f32[1088,128]{1,0:T(8,128)S(1)} %bitcast.6), custom_call_target="tpu_custom_call" | custom-call | tf_op jit(solution)/shard_map/pick/pallas_call | solution.py:209
  54.8 0.0 copy-start.1
  54.8 0.0 copy-start.2
  54.8 19.7 %all_to_all.11.tiles_ref = f32[16,136,128]{2,1,0:T(8,128)S(1)} all-to-all(f32[16,136,128]{2,1,0:T(8,128)S(1)} %pick.1), channel_id=1, replica_groups={{0,1,2,3,4,5,6,7,64,65,66,67,68,69,70,71},{8,9,10,11,12,13,14,15,72,73,..., dimensions={0} | all-to-all | bytes 2228224 | tf_op jit(solution)/shard_map/all_to_all | solution.py:218
  74.5 0.0 copy-done.1
  74.5 0.0 copy-done.2
  74.5 5.3 %solve.1 = f32[128,128]{1,0:T(8,128)} custom-call(f32[16,136,128]{2,1,0:T(8,128)S(1)} %all_to_all.11.tiles_ref, bf16[16,128,128]{2,1,0:T(8,128)(2,1)S(1)} %bitcast.7, f32[128,128]{1,0:T(8,128)S(1)} %copy-done.2), custom_call_target="tpu_custom_call" | custom-call | tf_op jit(solution)/shard_map/solve/pallas_call | solution.py:219
  (4 shorter events, 0.1 us)
Async XLA Ops:
  0.0 1.2 %copy-start = (f32[2048,128]{1,0:T(8,128)S(1)}, f32[2048,128]{1,0:T(8,128)}, u32[]{:S(2)}) copy-start(f32[2048,128]{1,0:T(8,128)} %shard_ref.1) | copy-start | bytes 3145732
  1.2 28.3 %copy-start.3 = (s32[1,16]{1,0:T(1,128)S(1)}, s32[1,16]{1,0:T(1,128)}, u32[]{:S(2)}) copy-start(s32[1,16]{1,0:T(1,128)} %param.5) | copy-start | bytes 196
  27.6 26.2 %collective-permute-start.5 = (f32[8,136,128]{2,1,0:T(8,128)S(1)}, f32[8,136,128]{2,1,0:T(8,128)S(1)}, u32[]{:S(2)}, u32[]{:S(2)}) collective-permute-start(f32[8,136,128]{2,1,0:T(8,128)S(1)} %all_to_all.10), channel_id=1, source_target_pairs={{0,32},{32,0},{64,96},{96,64},{128,160},{160,128},{192,224},{224,1... | collective-permute-start | bytes 1671176 | tf_op jit(solution)/shard_map/ppermute | solution.py:208
  29.5 5.5 %collective-permute-start = (s32[1,16]{1,0:T(1,128)S(1)}, s32[1,16]{1,0:T(1,128)S(1)}, u32[]{:S(2)}, u32[]{:S(2)}) collective-permute-start(s32[1,16]{1,0:T(1,128)S(1)} %copy-done.3), channel_id=1, source_target_pairs={{0,64},{32,96},{64,0},{96,32},{128,192},{160,224},{192,128},{224,1... | collective-permute-start | bytes 200 | tf_op jit(solution)/shard_map/ppermute | solution.py:182
  35.0 9.8 %collective-permute-start.3 = (s32[2,16]{1,0:T(2,128)S(1)}, s32[2,16]{1,0:T(2,128)S(1)}, u32[]{:S(2)}, u32[]{:S(2)}) collective-permute-start(s32[2,16]{1,0:T(2,128)S(1)} %pad_add_fusion), channel_id=1, source_target_pairs={{0,3},{1,2},{2,1},{3,0},{4,7},{5,6},{6,5},{7,4},{8,11},{9,10},{10,... | collective-permute-start | bytes 392 | tf_op jit(solution)/shard_map/ppermute | solution.py:199
  39.6 7.0 %collective-permute-start.2 = (s32[2,16]{1,0:T(2,128)S(1)}, s32[2,16]{1,0:T(2,128)S(1)}, u32[]{:S(2)}, u32[]{:S(2)}) collective-permute-start(s32[2,16]{1,0:T(2,128)S(1)} %pad_add_fusion), channel_id=1, source_target_pairs={{0,2},{1,3},{2,0},{3,1},{4,6},{5,7},{6,4},{7,5},{8,10},{9,11},{10,... | collective-permute-start | bytes 392 | tf_op jit(solution)/shard_map/ppermute | solution.py:199
  42.4 5.5 %collective-permute-start.1 = (s32[2,16]{1,0:T(2,128)S(1)}, s32[2,16]{1,0:T(2,128)S(1)}, u32[]{:S(2)}, u32[]{:S(2)}) collective-permute-start(s32[2,16]{1,0:T(2,128)S(1)} %pad_add_fusion), channel_id=1, source_target_pairs={{0,1},{1,0},{2,3},{3,2},{4,5},{5,4},{6,7},{7,6},{8,9},{9,8},{10,11... | collective-permute-start | bytes 392 | tf_op jit(solution)/shard_map/ppermute | solution.py:199
  47.8 5.8 %collective-permute-start.4 = (s32[8,16]{1,0:T(8,128)S(1)}, s32[8,16]{1,0:T(8,128)S(1)}, u32[]{:S(2)}, u32[]{:S(2)}) collective-permute-start(s32[8,16]{1,0:T(8,128)S(1)} %concatenate.12), channel_id=1, source_target_pairs={{0,4},{1,5},{2,6},{3,7},{4,0},{5,1},{6,2},{7,3},{8,12},{9,13},{10,... | collective-permute-start | bytes 1544 | tf_op jit(solution)/shard_map/ppermute | solution.py:203
  54.8 19.7 %copy-start.1 = (bf16[1,16,128,128]{3,2,1,0:T(8,128)(2,1)S(1)}, bf16[1,16,128,128]{3,2,1,0:T(8,128)(2,1)}, u32[]{:S(2)}) copy-start(bf16[1,16,128,128]{3,2,1,0:T(8,128)(2,1)} %param.6) | copy-start | bytes 1572868
  54.8 19.7 %copy-start.2 = (f32[128,128]{1,0:T(8,128)S(1)}, f32[128,128]{1,0:T(8,128)}, u32[]{:S(2)}) copy-start(f32[128,128]{1,0:T(8,128)} %start_ref.1) | copy-start | bytes 196612

commit v6 on v5

--- a/solution.py
+++ b/solution.py
@@ -69,6 +69,10 @@
         return 0
 
     lax.fori_loop(0, near, one, 0)
+
+
+def relay_kernel(lists_ref, out_ref):
+    out_ref[...] = lists_ref[...]
 
 
 def solve_kernel(tiles_ref, weights_ref, start_ref, out_ref, y_ref, resid_ref, dir_ref):
@@ -178,6 +182,15 @@
     place = (((item >> 1) & 1) * PLANE + (user & (PLANE - 1))).reshape(1)
     held = item_factors.shape[0] // TILE
 
+    tile_lists = pl.pallas_call(
+        relay_kernel,
+        out_shape=jax.ShapeDtypeStruct(tile_lists.shape, tile_lists.dtype),
+        in_specs=[VMEM],
+        out_specs=VMEM,
+        cost_estimate=pl.CostEstimate(flops=4 << 30, bytes_accessed=8 << 20, transcendentals=0),
+        compiler_params=grant(4),
+        name="relay",
+    )(tile_lists)
     pair_lists = jnp.concatenate(
         [tile_lists, lax.ppermute(tile_lists, "item", [(i, i ^ 2) for i in range(shards)])], axis=0
     )
@@ -226,7 +239,7 @@
             pltpu.VMEM((TILE, rank), jnp.float32),
             pltpu.VMEM((TILE, rank), jnp.float32),
         ],
-        compiler_params=grant(24),
+        compiler_params=pltpu.CompilerParams(vmem_limit_bytes=24 << 20),
         name="solve",
     )(tiles, tile_weights[0], user_factors)
 

time: 80.2 us -> 80.2 us (level)
  no operation moved by 1% of the time
where the time goes in v6:
time: 80.2 us; the launch traced here: 79.8 us
  blocking collectives  44.7 us (56%)
  starting transfers between devices  18.5 us (23%)
  Pallas kernels  7.62 us (10%)
  waiting for transfers between devices  7.55 us (9%)
  local copies, waits for them, and re-layouts  1.28 us (2%)
    all_to_all x1, blocking collectives, chain(): lax.all_to_all(send_a, 'item', 0, 0, tiled=True, axis_index_groups=column)  25.1 us
    all_to_all x1, blocking collectives, chain(): lax.all_to_all(send_b, ('item', 'user'), 0, 0, tiled=True, axis_index_gro...  19.7 us
    ppermute x3, starting transfers between devices, chain(): lax.ppermute(pair_lists, 'user', [(u, u ^ x) for u in range(users)])  9.81 us
    pallas_call x1, Pallas kernels, chain(): pl.pallas_call(solve_kernel, out_shape=jax.ShapeDtypeStruct((TILE, rank),...  5.33 us
    ppermute x1, starting transfers between devices, chain(): lax.ppermute(quad, 'user', [(u, u ^ 4) for u in range(users)])  4.27 us
    ppermute x3, waiting for transfers between devices, chain(): lax.ppermute(pair_lists, 'user', [(u, u ^ x) for u in range(users)])  3.01 us
    ppermute x1, waiting for transfers between devices, chain(): lax.ppermute(tile_lists, 'item', [(i, i ^ 2) for i in range(shards)])  2.98 us
    ppermute x1, starting transfers between devices, chain(): lax.ppermute(tile_lists, 'item', [(i, i ^ 2) for i in range(shards)])  2.47 us
  transfers between devices with their start and end apart: 6, of which 4 were waited for; matrix products, arithmetic and copies ran while one was open for 0% of the time, Pallas kernels for 0%

profile of v6, /device:TPU:128, one launch (start us, length us, event | category | flops | bytes accessed | tf_op | source)
XLA Modules:
  0.0 79.8 jit_solution(5744782343339296165)
XLA Ops:
  0.0 0.0 copy-start
  0.0 1.2 %copy-done = f32[2048,128]{1,0:T(8,128)S(1)} copy-done((f32[2048,128]{1,0:T(8,128)S(1)}, f32[2048,128]{1,0:T(8,128)}, u32[]{:S(2)}) %copy-start) | copy-done | bytes 1048600
  1.2 0.0 copy-start.3
  1.2 1.2 %prep.1 = f32[8,136,128]{2,1,0:T(8,128)S(1)} custom-call(s32[1]{0:T(128)} %bitcast.1.place_ref, f32[2048,128]{1,0:T(8,128)S(1)} %copy-done), custom_call_target="tpu_custom_call" | custom-call | tf_op jit(solution)/shard_map/prep/pallas_call | solution.py:197
  2.5 25.1 %all_to_all.10 = f32[8,136,128]{2,1,0:T(8,128)S(1)} all-to-all(f32[8,136,128]{2,1,0:T(8,128)S(1)} %prep.1), channel_id=1, replica_groups={{0,64,128,192,256,320,384,448},{32,96,160,224,288,352,416,480},{1,65,12..., dimensions={0} | all-to-all | bytes 1114112 | tf_op jit(solution)/shard_map/all_to_all | solution.py:210
  27.6 1.9 %collective-permute-start.5 = (f32[8,136,128]{2,1,0:T(8,128)S(1)}, f32[8,136,128]{2,1,0:T(8,128)S(1)}, u32[]{:S(2)}, u32[]{:S(2)}) collective-permute-start(f32[8,136,128]{2,1,0:T(8,128)S(1)} %all_to_all.10), channel_id=1, source_target_pairs={{0,32},{32,0},{64,96},{96,64},{128,160},{160,128},{192,224},{224,1... | collective-permute-start | bytes 1671176 | tf_op jit(solution)/shard_map/ppermute | solution.py:221
  29.5 0.0 copy-done.3
  29.5 2.5 %collective-permute-start = (s32[1,16]{1,0:T(1,128)S(1)}, s32[1,16]{1,0:T(1,128)S(1)}, u32[]{:S(2)}, u32[]{:S(2)}) collective-permute-start(s32[1,16]{1,0:T(1,128)S(1)} %relay.1), channel_id=1, source_target_pairs={{0,64},{32,96},{64,0},{96,32},{128,192},{160,224},{192,128},{224,1... | collective-permute-start | bytes 200 | tf_op jit(solution)/shard_map/ppermute | solution.py:195
  32.0 3.0 %collective-permute-done = s32[1,16]{1,0:T(1,128)S(1)} collective-permute-done((s32[1,16]{1,0:T(1,128)S(1)}, s32[1,16]{1,0:T(1,128)S(1)}, u32[]{:S(2)}, u32[]{:S(2)}) %collective-permute-start) | collective-permute-done | bytes 96 | tf_op jit(solution)/shard_map/ppermute | solution.py:195
  35.0 4.7 %collective-permute-start.3 = (s32[2,16]{1,0:T(2,128)S(1)}, s32[2,16]{1,0:T(2,128)S(1)}, u32[]{:S(2)}, u32[]{:S(2)}) collective-permute-start(s32[2,16]{1,0:T(2,128)S(1)} %pad_add_fusion), channel_id=1, source_target_pairs={{0,3},{1,2},{2,1},{3,0},{4,7},{5,6},{6,5},{7,4},{8,11},{9,10},{10,... | collective-permute-start | bytes 392 | tf_op jit(solution)/shard_map/ppermute | solution.py:212
  39.6 2.7 %collective-permute-start.2 = (s32[2,16]{1,0:T(2,128)S(1)}, s32[2,16]{1,0:T(2,128)S(1)}, u32[]{:S(2)}, u32[]{:S(2)}) collective-permute-start(s32[2,16]{1,0:T(2,128)S(1)} %pad_add_fusion), channel_id=1, source_target_pairs={{0,2},{1,3},{2,0},{3,1},{4,6},{5,7},{6,4},{7,5},{8,10},{9,11},{10,... | collective-permute-start | bytes 392 | tf_op jit(solution)/shard_map/ppermute | solution.py:212
  42.4 2.4 %collective-permute-start.1 = (s32[2,16]{1,0:T(2,128)S(1)}, s32[2,16]{1,0:T(2,128)S(1)}, u32[]{:S(2)}, u32[]{:S(2)}) collective-permute-start(s32[2,16]{1,0:T(2,128)S(1)} %pad_add_fusion), channel_id=1, source_target_pairs={{0,1},{1,0},{2,3},{3,2},{4,5},{5,4},{6,7},{7,6},{8,9},{9,8},{10,11... | collective-permute-start | bytes 392 | tf_op jit(solution)/shard_map/ppermute | solution.py:212
  44.8 0.0 collective-permute-done.3
  44.8 1.8 %collective-permute-done.2 = s32[2,16]{1,0:T(2,128)S(1)} collective-permute-done((s32[2,16]{1,0:T(2,128)S(1)}, s32[2,16]{1,0:T(2,128)S(1)}, u32[]{:S(2)}, u32[]{:S(2)}) %collective-permute-start.2) | collective-permute-done | bytes 160 | tf_op jit(solution)/shard_map/ppermute | solution.py:212
  46.6 1.2 %collective-permute-done.1 = s32[2,16]{1,0:T(2,128)S(1)} collective-permute-done((s32[2,16]{1,0:T(2,128)S(1)}, s32[2,16]{1,0:T(2,128)S(1)}, u32[]{:S(2)}, u32[]{:S(2)}) %collective-permute-start.1) | collective-permute-done | bytes 160 | tf_op jit(solution)/shard_map/ppermute | solution.py:212
  47.9 4.3 %collective-permute-start.4 = (s32[8,16]{1,0:T(8,128)S(1)}, s32[8,16]{1,0:T(8,128)S(1)}, u32[]{:S(2)}, u32[]{:S(2)}) collective-permute-start(s32[8,16]{1,0:T(8,128)S(1)} %concatenate.12), channel_id=1, source_target_pairs={{0,4},{1,5},{2,6},{3,7},{4,0},{5,1},{6,2},{7,3},{8,12},{9,13},{10,... | collective-permute-start | bytes 1544 | tf_op jit(solution)/shard_map/ppermute | solution.py:216
  52.1 1.6 %collective-permute-done.4 = s32[8,16]{1,0:T(8,128)S(1)} collective-permute-done((s32[8,16]{1,0:T(8,128)S(1)}, s32[8,16]{1,0:T(8,128)S(1)}, u32[]{:S(2)}, u32[]{:S(2)}) %collective-permute-start.4) | collective-permute-done | bytes 544 | tf_op jit(solution)/shard_map/ppermute | solution.py:216
  53.8 0.0 collective-permute-done.5
  53.8 1.1 %pick.1 = f32[16,136,128]{2,1,0:T(8,128)S(1)} custom-call(s32[1]{0:T(128)} %bitcast.place_ref, s32[16,16]{1,0:T(8,128)S(1)} %fusion.4.at_ref, f32[1088,128]{1,0:T(8,128)S(1)} %bitcast.5, f32[1088,128]{1,0:T(8,128)S(1)} %bitcast.6), custom_call_target="tpu_custom_call" | custom-call | tf_op jit(solution)/shard_map/pick/pallas_call | solution.py:222
  54.8 0.0 copy-start.1
  54.8 0.0 copy-start.2
  54.8 19.7 %all_to_all.11.tiles_ref = f32[16,136,128]{2,1,0:T(8,128)S(1)} all-to-all(f32[16,136,128]{2,1,0:T(8,128)S(1)} %pick.1), channel_id=1, replica_groups={{0,1,2,3,4,5,6,7,64,65,66,67,68,69,70,71},{8,9,10,11,12,13,14,15,72,73,..., dimensions={0} | all-to-all | bytes 2228224 | tf_op jit(solution)/shard_map/all_to_all | solution.py:231
  74.5 0.0 copy-done.1
  74.5 0.0 copy-done.2
  74.5 5.3 %solve.1 = f32[128,128]{1,0:T(8,128)} custom-call(f32[16,136,128]{2,1,0:T(8,128)S(1)} %all_to_all.11.tiles_ref, bf16[16,128,128]{2,1,0:T(8,128)(2,1)S(1)} %bitcast.7, f32[128,128]{1,0:T(8,128)S(1)} %copy-done.2), custom_call_target="tpu_custom_call" | custom-call | tf_op jit(solution)/shard_map/solve/pallas_call | solution.py:232
  (5 shorter events, 0.1 us)
Async XLA Ops:
  0.0 1.2 %copy-start = (f32[2048,128]{1,0:T(8,128)S(1)}, f32[2048,128]{1,0:T(8,128)}, u32[]{:S(2)}) copy-start(f32[2048,128]{1,0:T(8,128)} %shard_ref.1) | copy-start | bytes 3145732
  1.2 28.3 %copy-start.3 = (s32[1,16]{1,0:T(1,128)S(1)}, s32[1,16]{1,0:T(1,128)}, u32[]{:S(2)}) copy-start(s32[1,16]{1,0:T(1,128)} %lists_ref.1) | copy-start | bytes 196
  27.6 26.2 %collective-permute-start.5 = (f32[8,136,128]{2,1,0:T(8,128)S(1)}, f32[8,136,128]{2,1,0:T(8,128)S(1)}, u32[]{:S(2)}, u32[]{:S(2)}) collective-permute-start(f32[8,136,128]{2,1,0:T(8,128)S(1)} %all_to_all.10), channel_id=1, source_target_pairs={{0,32},{32,0},{64,96},{96,64},{128,160},{160,128},{192,224},{224,1... | collective-permute-start | bytes 1671176 | tf_op jit(solution)/shard_map/ppermute | solution.py:221
  29.5 5.5 %collective-permute-start = (s32[1,16]{1,0:T(1,128)S(1)}, s32[1,16]{1,0:T(1,128)S(1)}, u32[]{:S(2)}, u32[]{:S(2)}) collective-permute-start(s32[1,16]{1,0:T(1,128)S(1)} %relay.1), channel_id=1, source_target_pairs={{0,64},{32,96},{64,0},{96,32},{128,192},{160,224},{192,128},{224,1... | collective-permute-start | bytes 200 | tf_op jit(solution)/shard_map/ppermute | solution.py:195
  35.0 9.8 %collective-permute-start.3 = (s32[2,16]{1,0:T(2,128)S(1)}, s32[2,16]{1,0:T(2,128)S(1)}, u32[]{:S(2)}, u32[]{:S(2)}) collective-permute-start(s32[2,16]{1,0:T(2,128)S(1)} %pad_add_fusion), channel_id=1, source_target_pairs={{0,3},{1,2},{2,1},{3,0},{4,7},{5,6},{6,5},{7,4},{8,11},{9,10},{10,... | collective-permute-start | bytes 392 | tf_op jit(solution)/shard_map/ppermute | solution.py:212
  39.6 7.0 %collective-permute-start.2 = (s32[2,16]{1,0:T(2,128)S(1)}, s32[2,16]{1,0:T(2,128)S(1)}, u32[]{:S(2)}, u32[]{:S(2)}) collective-permute-start(s32[2,16]{1,0:T(2,128)S(1)} %pad_add_fusion), channel_id=1, source_target_pairs={{0,2},{1,3},{2,0},{3,1},{4,6},{5,7},{6,4},{7,5},{8,10},{9,11},{10,... | collective-permute-start | bytes 392 | tf_op jit(solution)/shard_map/ppermute | solution.py:212
  42.4 5.5 %collective-permute-start.1 = (s32[2,16]{1,0:T(2,128)S(1)}, s32[2,16]{1,0:T(2,128)S(1)}, u32[]{:S(2)}, u32[]{:S(2)}) collective-permute-start(s32[2,16]{1,0:T(2,128)S(1)} %pad_add_fusion), channel_id=1, source_target_pairs={{0,1},{1,0},{2,3},{3,2},{4,5},{5,4},{6,7},{7,6},{8,9},{9,8},{10,11... | collective-permute-start | bytes 392 | tf_op jit(solution)/shard_map/ppermute | solution.py:212
  47.9 5.8 %collective-permute-start.4 = (s32[8,16]{1,0:T(8,128)S(1)}, s32[8,16]{1,0:T(8,128)S(1)}, u32[]{:S(2)}, u32[]{:S(2)}) collective-permute-start(s32[8,16]{1,0:T(8,128)S(1)} %concatenate.12), channel_id=1, source_target_pairs={{0,4},{1,5},{2,6},{3,7},{4,0},{5,1},{6,2},{7,3},{8,12},{9,13},{10,... | collective-permute-start | bytes 1544 | tf_op jit(solution)/shard_map/ppermute | solution.py:216
  54.8 19.7 %copy-start.1 = (bf16[1,16,128,128]{3,2,1,0:T(8,128)(2,1)S(1)}, bf16[1,16,128,128]{3,2,1,0:T(8,128)(2,1)}, u32[]{:S(2)}) copy-start(bf16[1,16,128,128]{3,2,1,0:T(8,128)(2,1)} %param.6) | copy-start | bytes 1572868
  54.8 19.7 %copy-start.2 = (f32[128,128]{1,0:T(8,128)S(1)}, f32[128,128]{1,0:T(8,128)}, u32[]{:S(2)}) copy-start(f32[128,128]{1,0:T(8,128)} %start_ref.1) | copy-start | bytes 196612

commit v7 on v5

--- a/solution.py
+++ b/solution.py
@@ -27,7 +27,7 @@
     return (x[:rows, :cols] + x[:rows, cols:]) + (x[rows:, :cols] + x[rows:, cols:])
 
 
-def prep_kernel(place_ref, shard_ref, out_ref, stage_ref, gram_ref, out_sem):
+def prep_kernel(place_ref, ticket_ref, shard_ref, out_ref, stage_ref, gram_ref, out_sem):
     rows = shard_ref.shape[0]
     tiles = rows // TILE
     body, tail = pl.ds(0, tiles * SLICE), pl.ds(tiles * SLICE, SLICE)
@@ -71,7 +71,11 @@
     lax.fori_loop(0, near, one, 0)
 
 
-def solve_kernel(tiles_ref, weights_ref, start_ref, out_ref, y_ref, resid_ref, dir_ref):
+def ahead_kernel(out_ref):
+    out_ref[...] = jnp.zeros_like(out_ref)
+
+
+def solve_kernel(tiles_ref, weights_ref, start_ref, out_ref, y_ref, resid_ref, dir_ref, part_ref):
     near = tiles_ref.shape[0]
     slots = weights_ref.shape[0]
     items = slots * TILE
@@ -110,14 +114,11 @@
         return (g[:TILE] + g[TILE:]) + RIDGE_WEIGHT * v
 
     def gathered(left, of):
-        total = None
         for n in range(items // chunk):
-            part = jnp.dot(
-                jnp.concatenate(halves(of(scores(left, n), wide(n))), axis=0),
-                y_ref[n * chunk:(n + 1) * chunk, :],
-                preferred_element_type=jnp.float32,
+            part_ref[:, n * chunk:(n + 1) * chunk] = jnp.concatenate(
+                halves(of(scores(left, n), wide(n))), axis=0
             )
-            total = part if total is None else total + part
+        total = jnp.dot(part_ref[...], y_ref[:items, :], preferred_element_type=jnp.float32)
         return quadrants(total)
 
     start = start_ref[...]
@@ -178,13 +179,21 @@
     place = (((item >> 1) & 1) * PLANE + (user & (PLANE - 1))).reshape(1)
     held = item_factors.shape[0] // TILE
 
+    ticket = pl.pallas_call(
+        ahead_kernel,
+        out_shape=jax.ShapeDtypeStruct((8, rank), jnp.float32),
+        out_specs=VMEM,
+        cost_estimate=pl.CostEstimate(flops=4 << 30, bytes_accessed=8 << 20, transcendentals=0),
+        compiler_params=grant(4),
+        name="ahead",
+    )()
     pair_lists = jnp.concatenate(
         [tile_lists, lax.ppermute(tile_lists, "item", [(i, i ^ 2) for i in range(shards)])], axis=0
     )
     send_a = pl.pallas_call(
         prep_kernel,
         out_shape=jax.ShapeDtypeStruct((ROWS, (held + 1) * SLICE, rank), jnp.float32),
-        in_specs=[SMEM, VMEM],
+        in_specs=[SMEM, VMEM, VMEM],
         out_specs=pl.BlockSpec(memory_space=pltpu.MemorySpace.HBM),
         scratch_shapes=[
             pltpu.VMEM((2, (held + 1) * SLICE, rank), jnp.float32),
@@ -193,7 +202,7 @@
         ],
         compiler_params=grant(16),
         name="prep",
-    )(beside, item_factors)
+    )(beside, ticket, item_factors)
     mine = lax.all_to_all(send_a, "item", 0, 0, tiled=True, axis_index_groups=column)
     quad = [pair_lists] + [
         lax.ppermute(pair_lists, "user", [(u, u ^ x) for u in range(users)]) for x in range(1, 4)
@@ -225,8 +234,9 @@
             pltpu.VMEM(((slots + 1) * TILE, 2 * rank), jnp.bfloat16),
             pltpu.VMEM((TILE, rank), jnp.float32),
             pltpu.VMEM((TILE, rank), jnp.float32),
+            pltpu.VMEM((2 * TILE, slots * TILE), jnp.bfloat16),
         ],
-        compiler_params=grant(24),
+        compiler_params=pltpu.CompilerParams(vmem_limit_bytes=24 << 20),
         name="solve",
     )(tiles, tile_weights[0], user_factors)
 

time: 80.2 us -> 80.3 us (level)
  no operation moved by 1% of the time
where the time goes in v7:
time: 80.3 us; the launch traced here: 79.9 us
  blocking collectives  44.7 us (56%)
  starting transfers between devices  18.5 us (23%)
  Pallas kernels  7.71 us (10%)
  waiting for transfers between devices  7.56 us (9%)
  local copies, waits for them, and re-layouts  1.28 us (2%)
    all_to_all x1, blocking collectives, chain(): lax.all_to_all(send_a, 'item', 0, 0, tiled=True, axis_index_groups=column)  25.1 us
    all_to_all x1, blocking collectives, chain(): lax.all_to_all(send_b, ('item', 'user'), 0, 0, tiled=True, axis_index_gro...  19.6 us
    ppermute x3, starting transfers between devices, chain(): lax.ppermute(pair_lists, 'user', [(u, u ^ x) for u in range(users)])  9.81 us
    pallas_call x1, Pallas kernels, chain(): pl.pallas_call(solve_kernel, out_shape=jax.ShapeDtypeStruct((TILE, rank),...  5.43 us
    ppermute x1, starting transfers between devices, chain(): lax.ppermute(quad, 'user', [(u, u ^ 4) for u in range(users)])  4.27 us
    ppermute x3, waiting for transfers between devices, chain(): lax.ppermute(pair_lists, 'user', [(u, u ^ x) for u in range(users)])  3.01 us
    ppermute x1, waiting for transfers between devices, chain(): lax.ppermute(tile_lists, 'item', [(i, i ^ 2) for i in range(shards)])  2.98 us
    ppermute x1, starting transfers between devices, chain(): lax.ppermute(tile_lists, 'item', [(i, i ^ 2) for i in range(shards)])  2.47 us
  transfers between devices with their start and end apart: 6, of which 4 were waited for; matrix products, arithmetic and copies ran while one was open for 0% of the time, Pallas kernels for 0%

profile of v7, /device:TPU:128, one launch (start us, length us, event | category | flops | bytes accessed | tf_op | source)
XLA Modules:
  0.0 79.9 jit_solution(18037800500188153414)
XLA Ops:
  0.0 0.0 copy-start
  0.0 1.2 %copy-done = f32[2048,128]{1,0:T(8,128)S(1)} copy-done((f32[2048,128]{1,0:T(8,128)S(1)}, f32[2048,128]{1,0:T(8,128)}, u32[]{:S(2)}) %copy-start) | copy-done | bytes 1048600
  1.2 0.0 copy-start.3
  1.2 1.2 %prep.1 = f32[8,136,128]{2,1,0:T(8,128)S(1)} custom-call(s32[1]{0:T(128)} %bitcast.1.place_ref, f32[8,128]{1,0:T(8,128)S(1)} %ahead.1.ticket_ref, f32[2048,128]{1,0:T(8,128)S(1)} %copy-done), custom_call_target="tpu_custom_call" | custom-call | tf_op jit(solution)/shard_map/prep/pallas_call | solution.py:193
  2.5 25.1 %all_to_all.10 = f32[8,136,128]{2,1,0:T(8,128)S(1)} all-to-all(f32[8,136,128]{2,1,0:T(8,128)S(1)} %prep.1), channel_id=1, replica_groups={{0,64,128,192,256,320,384,448},{32,96,160,224,288,352,416,480},{1,65,12..., dimensions={0} | all-to-all | bytes 1114112 | tf_op jit(solution)/shard_map/all_to_all | solution.py:206
  27.6 1.9 %collective-permute-start.5 = (f32[8,136,128]{2,1,0:T(8,128)S(1)}, f32[8,136,128]{2,1,0:T(8,128)S(1)}, u32[]{:S(2)}, u32[]{:S(2)}) collective-permute-start(f32[8,136,128]{2,1,0:T(8,128)S(1)} %all_to_all.10), channel_id=1, source_target_pairs={{0,32},{32,0},{64,96},{96,64},{128,160},{160,128},{192,224},{224,1... | collective-permute-start | bytes 1671176 | tf_op jit(solution)/shard_map/ppermute | solution.py:217
  29.5 0.0 copy-done.3
  29.5 2.5 %collective-permute-start = (s32[1,16]{1,0:T(1,128)S(1)}, s32[1,16]{1,0:T(1,128)S(1)}, u32[]{:S(2)}, u32[]{:S(2)}) collective-permute-start(s32[1,16]{1,0:T(1,128)S(1)} %copy-done.3), channel_id=1, source_target_pairs={{0,64},{32,96},{64,0},{96,32},{128,192},{160,224},{192,128},{224,1... | collective-permute-start | bytes 200 | tf_op jit(solution)/shard_map/ppermute | solution.py:191
  32.0 3.0 %collective-permute-done = s32[1,16]{1,0:T(1,128)S(1)} collective-permute-done((s32[1,16]{1,0:T(1,128)S(1)}, s32[1,16]{1,0:T(1,128)S(1)}, u32[]{:S(2)}, u32[]{:S(2)}) %collective-permute-start) | collective-permute-done | bytes 96 | tf_op jit(solution)/shard_map/ppermute | solution.py:191
  35.0 4.7 %collective-permute-start.3 = (s32[2,16]{1,0:T(2,128)S(1)}, s32[2,16]{1,0:T(2,128)S(1)}, u32[]{:S(2)}, u32[]{:S(2)}) collective-permute-start(s32[2,16]{1,0:T(2,128)S(1)} %pad_add_fusion), channel_id=1, source_target_pairs={{0,3},{1,2},{2,1},{3,0},{4,7},{5,6},{6,5},{7,4},{8,11},{9,10},{10,... | collective-permute-start | bytes 392 | tf_op jit(solution)/shard_map/ppermute | solution.py:208
  39.6 2.7 %collective-permute-start.2 = (s32[2,16]{1,0:T(2,128)S(1)}, s32[2,16]{1,0:T(2,128)S(1)}, u32[]{:S(2)}, u32[]{:S(2)}) collective-permute-start(s32[2,16]{1,0:T(2,128)S(1)} %pad_add_fusion), channel_id=1, source_target_pairs={{0,2},{1,3},{2,0},{3,1},{4,6},{5,7},{6,4},{7,5},{8,10},{9,11},{10,... | collective-permute-start | bytes 392 | tf_op jit(solution)/shard_map/ppermute | solution.py:208
  42.3 2.4 %collective-permute-start.1 = (s32[2,16]{1,0:T(2,128)S(1)}, s32[2,16]{1,0:T(2,128)S(1)}, u32[]{:S(2)}, u32[]{:S(2)}) collective-permute-start(s32[2,16]{1,0:T(2,128)S(1)} %pad_add_fusion), channel_id=1, source_target_pairs={{0,1},{1,0},{2,3},{3,2},{4,5},{5,4},{6,7},{7,6},{8,9},{9,8},{10,11... | collective-permute-start | bytes 392 | tf_op jit(solution)/shard_map/ppermute | solution.py:208
  44.8 0.0 collective-permute-done.3
  44.8 1.8 %collective-permute-done.2 = s32[2,16]{1,0:T(2,128)S(1)} collective-permute-done((s32[2,16]{1,0:T(2,128)S(1)}, s32[2,16]{1,0:T(2,128)S(1)}, u32[]{:S(2)}, u32[]{:S(2)}) %collective-permute-start.2) | collective-permute-done | bytes 160 | tf_op jit(solution)/shard_map/ppermute | solution.py:208
  46.6 1.2 %collective-permute-done.1 = s32[2,16]{1,0:T(2,128)S(1)} collective-permute-done((s32[2,16]{1,0:T(2,128)S(1)}, s32[2,16]{1,0:T(2,128)S(1)}, u32[]{:S(2)}, u32[]{:S(2)}) %collective-permute-start.1) | collective-permute-done | bytes 160 | tf_op jit(solution)/shard_map/ppermute | solution.py:208
  47.8 4.3 %collective-permute-start.4 = (s32[8,16]{1,0:T(8,128)S(1)}, s32[8,16]{1,0:T(8,128)S(1)}, u32[]{:S(2)}, u32[]{:S(2)}) collective-permute-start(s32[8,16]{1,0:T(8,128)S(1)} %concatenate.12), channel_id=1, source_target_pairs={{0,4},{1,5},{2,6},{3,7},{4,0},{5,1},{6,2},{7,3},{8,12},{9,13},{10,... | collective-permute-start | bytes 1544 | tf_op jit(solution)/shard_map/ppermute | solution.py:212
  52.1 1.6 %collective-permute-done.4 = s32[8,16]{1,0:T(8,128)S(1)} collective-permute-done((s32[8,16]{1,0:T(8,128)S(1)}, s32[8,16]{1,0:T(8,128)S(1)}, u32[]{:S(2)}, u32[]{:S(2)}) %collective-permute-start.4) | collective-permute-done | bytes 544 | tf_op jit(solution)/shard_map/ppermute | solution.py:212
  53.7 0.0 collective-permute-done.5
  53.7 1.1 %pick.1 = f32[16,136,128]{2,1,0:T(8,128)S(1)} custom-call(s32[1]{0:T(128)} %bitcast.place_ref, s32[16,16]{1,0:T(8,128)S(1)} %fusion.4.at_ref, f32[1088,128]{1,0:T(8,128)S(1)} %bitcast.5, f32[1088,128]{1,0:T(8,128)S(1)} %bitcast.6), custom_call_target="tpu_custom_call" | custom-call | tf_op jit(solution)/shard_map/pick/pallas_call | solution.py:218
  54.8 0.0 copy-start.1
  54.8 0.0 copy-start.2
  54.8 19.6 %all_to_all.11.tiles_ref = f32[16,136,128]{2,1,0:T(8,128)S(1)} all-to-all(f32[16,136,128]{2,1,0:T(8,128)S(1)} %pick.1), channel_id=1, replica_groups={{0,1,2,3,4,5,6,7,64,65,66,67,68,69,70,71},{8,9,10,11,12,13,14,15,72,73,..., dimensions={0} | all-to-all | bytes 2228224 | tf_op jit(solution)/shard_map/all_to_all | solution.py:227
  74.5 0.0 copy-done.1
  74.5 0.0 copy-done.2
  74.5 5.4 %solve.1 = f32[128,128]{1,0:T(8,128)} custom-call(f32[16,136,128]{2,1,0:T(8,128)S(1)} %all_to_all.11.tiles_ref, bf16[16,128,128]{2,1,0:T(8,128)(2,1)S(1)} %bitcast.7, f32[128,128]{1,0:T(8,128)S(1)} %copy-done.2), custom_call_target="tpu_custom_call" | custom-call | tf_op jit(solution)/shard_map/solve/pallas_call | solution.py:228
  (5 shorter events, 0.1 us)
Async XLA Ops:
  0.0 1.2 %copy-start = (f32[2048,128]{1,0:T(8,128)S(1)}, f32[2048,128]{1,0:T(8,128)}, u32[]{:S(2)}) copy-start(f32[2048,128]{1,0:T(8,128)} %shard_ref.1) | copy-start | bytes 3145732
  1.2 28.3 %copy-start.3 = (s32[1,16]{1,0:T(1,128)S(1)}, s32[1,16]{1,0:T(1,128)}, u32[]{:S(2)}) copy-start(s32[1,16]{1,0:T(1,128)} %param.5) | copy-start | bytes 196
  27.6 26.2 %collective-permute-start.5 = (f32[8,136,128]{2,1,0:T(8,128)S(1)}, f32[8,136,128]{2,1,0:T(8,128)S(1)}, u32[]{:S(2)}, u32[]{:S(2)}) collective-permute-start(f32[8,136,128]{2,1,0:T(8,128)S(1)} %all_to_all.10), channel_id=1, source_target_pairs={{0,32},{32,0},{64,96},{96,64},{128,160},{160,128},{192,224},{224,1... | collective-permute-start | bytes 1671176 | tf_op jit(solution)/shard_map/ppermute | solution.py:217
  29.5 5.5 %collective-permute-start = (s32[1,16]{1,0:T(1,128)S(1)}, s32[1,16]{1,0:T(1,128)S(1)}, u32[]{:S(2)}, u32[]{:S(2)}) collective-permute-start(s32[1,16]{1,0:T(1,128)S(1)} %copy-done.3), channel_id=1, source_target_pairs={{0,64},{32,96},{64,0},{96,32},{128,192},{160,224},{192,128},{224,1... | collective-permute-start | bytes 200 | tf_op jit(solution)/shard_map/ppermute | solution.py:191
  35.0 9.8 %collective-permute-start.3 = (s32[2,16]{1,0:T(2,128)S(1)}, s32[2,16]{1,0:T(2,128)S(1)}, u32[]{:S(2)}, u32[]{:S(2)}) collective-permute-start(s32[2,16]{1,0:T(2,128)S(1)} %pad_add_fusion), channel_id=1, source_target_pairs={{0,3},{1,2},{2,1},{3,0},{4,7},{5,6},{6,5},{7,4},{8,11},{9,10},{10,... | collective-permute-start | bytes 392 | tf_op jit(solution)/shard_map/ppermute | solution.py:208
  39.6 7.0 %collective-permute-start.2 = (s32[2,16]{1,0:T(2,128)S(1)}, s32[2,16]{1,0:T(2,128)S(1)}, u32[]{:S(2)}, u32[]{:S(2)}) collective-permute-start(s32[2,16]{1,0:T(2,128)S(1)} %pad_add_fusion), channel_id=1, source_target_pairs={{0,2},{1,3},{2,0},{3,1},{4,6},{5,7},{6,4},{7,5},{8,10},{9,11},{10,... | collective-permute-start | bytes 392 | tf_op jit(solution)/shard_map/ppermute | solution.py:208
  42.3 5.5 %collective-permute-start.1 = (s32[2,16]{1,0:T(2,128)S(1)}, s32[2,16]{1,0:T(2,128)S(1)}, u32[]{:S(2)}, u32[]{:S(2)}) collective-permute-start(s32[2,16]{1,0:T(2,128)S(1)} %pad_add_fusion), channel_id=1, source_target_pairs={{0,1},{1,0},{2,3},{3,2},{4,5},{5,4},{6,7},{7,6},{8,9},{9,8},{10,11... | collective-permute-start | bytes 392 | tf_op jit(solution)/shard_map/ppermute | solution.py:208
  47.8 5.9 %collective-permute-start.4 = (s32[8,16]{1,0:T(8,128)S(1)}, s32[8,16]{1,0:T(8,128)S(1)}, u32[]{:S(2)}, u32[]{:S(2)}) collective-permute-start(s32[8,16]{1,0:T(8,128)S(1)} %concatenate.12), channel_id=1, source_target_pairs={{0,4},{1,5},{2,6},{3,7},{4,0},{5,1},{6,2},{7,3},{8,12},{9,13},{10,... | collective-permute-start | bytes 1544 | tf_op jit(solution)/shard_map/ppermute | solution.py:212
  54.8 19.7 %copy-start.1 = (bf16[1,16,128,128]{3,2,1,0:T(8,128)(2,1)S(1)}, bf16[1,16,128,128]{3,2,1,0:T(8,128)(2,1)}, u32[]{:S(2)}) copy-start(bf16[1,16,128,128]{3,2,1,0:T(8,128)(2,1)} %param.6) | copy-start | bytes 1572868
  54.8 19.7 %copy-start.2 = (f32[128,128]{1,0:T(8,128)S(1)}, f32[128,128]{1,0:T(8,128)}, u32[]{:S(2)}) copy-start(f32[128,128]{1,0:T(8,128)} %start_ref.1) | copy-start | bytes 196612
